TPU v7x, 256 devices: a whole 4x4x8 slice. The times are simulated.
256 devices in a mesh: seq: 64 (over z, y, core), tensor: 4 (over x).
Axes of the slice: x: 4, y: 4, z: 8, core: 2. Of those that a mesh axis runs over, the one named last changes fastest.
Arguments:
- tokens: bfloat16 [32768, 2048], P('seq', 'tensor')
- norm_gain: float32 [2048], replicated, may hold values from 0.5 to 1.5
- w_qkv: bfloat16 [2048, 4, 1024], P(None, 'tensor'), may hold values from -0.125 to 0.125
- w_gate_out: bfloat16 [2048, 2048], P(None, 'tensor'), may hold values from -0.125 to 0.125
- gate_down: bfloat16 [2048, 16], replicated
- gate_up: float32 [16, 4, 256], P(None, 'tensor')
- gate_bias: float32 [4, 256], P('tensor')
- conv_weight: float32 [4, 4, 1024], P(None, 'tensor'), may hold values from -3 to 3
- head_gain: float32 [512], replicated, may hold values from 0.5 to 1.5
- w_out: bfloat16 [2048, 2048], P('tensor'), may hold values from -0.125 to 0.125
- spans: int32 [3], replicated, may hold values from 1 to 48, 64 in all
- fills: int32 [3], replicated, may hold values from 1 to 512
- request_prompt: int32 [128], P('seq'), may hold values from -1 to 2, as said below
Outputs:
- mixed: bfloat16 [32768, 2048], P(('seq', 'tensor'))
- owner_state: float32 [128, 4, 256, 512], P('seq', 'tensor')
- owner_edge: bfloat16 [128, 3, 4, 1024], P('seq', None, 'tensor')
Inputs may be any that keep to these rules, and one draw needn't show every extreme that they name: `spans`: the prompts lie along seq in order and together cover all its indices. `request_prompt`: slots r * 2 to r * 2 + 1 belong to index r of seq; the first slot of every index names a prompt; every prompt is named by some slot.
All inputs are finite; a program needn't handle non-finite values.
Results may differ from a plain program's by a relative error of at most 0.0095.
Values may be sent and summed in bfloat16 or wider, within the bound.
A program may use at most 128 MiB of HBM per device.

v0:
```python
import jax
import jax.numpy as jnp
from jax import lax
from jax.sharding import PartitionSpec as P

STRETCH = 64


EPS_IN = 1e-06
EPS_HEAD = 1e-05
EXACT_MATMUL = lax.Precision.HIGHEST


def from_behind(array, axis, by):
    peers = lax.axis_size(axis)
    pairs = [(i, i + by) for i in range(peers) if 0 <= i + by < peers]
    return lax.ppermute(array, axis, pairs)


def broadcast(block, axis, source):
    block = jnp.where(lax.axis_index(axis) == source, block, jnp.zeros_like(block))
    return lax.psum(block, axis)


def block_pass(carry, pieces):
    passed_along_state, offset = carry
    q_blk, k_blk, value_block, decay_blk = pieces
    block_rows = q_blk.shape[0]
    k_wide = k_blk.astype(jnp.float32)
    cumulative = jnp.cumsum(decay_blk, axis=0)
    query_decayed = (q_blk * jnp.exp(cumulative)).astype(jnp.bfloat16)
    pair_decay = jnp.exp(jnp.minimum(cumulative[:, None] - cumulative[None, :], 0.0))
    causal_mask = jnp.arange(block_rows)[:, None] >= jnp.arange(block_rows)[None, :]
    scores = jnp.einsum("ihk,jhk,ijhk->hij", q_blk, k_wide, pair_decay, precision=EXACT_MATMUL)
    scores = jnp.where(causal_mask[None], scores, 0.0).astype(jnp.bfloat16)
    intra_term = jnp.einsum("hij,jhv->ihv", scores, value_block, preferred_element_type=jnp.float32)
    closing_decay = cumulative[-1]
    weight_applied = (k_wide * jnp.exp(closing_decay[None] - cumulative)).astype(jnp.bfloat16)
    updated = jnp.exp(closing_decay)[:, :, None] * passed_along_state + jnp.einsum(
        "qbr,qbp->brp", weight_applied, value_block, preferred_element_type=jnp.float32
    )
    return (
        (updated, offset + closing_decay),
        (intra_term, passed_along_state, offset, query_decayed),
    )


def body(
    tokens,
    norm_gain,
    w_qkv,
    w_gate_out,
    gate_down,
    gate_up,
    gate_bias,
    conv_weight,
    head_gain,
    w_out,
    spans,
    fills,
    request_prompt,
):
    row_count = tokens.shape[0]
    local_heads = w_qkv.shape[1]
    width_qkv = w_qkv.shape[2]
    key_width = gate_up.shape[2]
    value_width = head_gain.shape[0]
    model_width = norm_gain.shape[0]
    taps = conv_weight.shape[0]
    prompts = spans.shape[0]
    slot_count = request_prompt.shape[0]
    seq_index = lax.axis_index("seq")
    span_ends = jnp.cumsum(spans)
    starts = span_ends - spans
    my_prompt = jnp.sum((span_ends <= seq_index).astype(jnp.int32))
    picked = jnp.arange(prompts, dtype=jnp.int32) == my_prompt
    first_dev = jnp.sum(jnp.where(picked, starts, 0))
    last_dev = jnp.sum(jnp.where(picked, span_ends - 1, 0))
    is_start = seq_index == first_dev
    is_last = seq_index == last_dev
    live_rows = jnp.where(is_last, jnp.sum(jnp.where(picked, fills, 0)), row_count)
    valid = jnp.arange(row_count, dtype=jnp.int32) < live_rows
    value_entries = tokens.astype(jnp.float32)
    squares = lax.psum(jnp.sum(value_entries * value_entries, axis=1), "tensor")
    inverse = lax.rsqrt(squares / model_width + EPS_IN)
    flat_qkv = w_qkv.reshape(model_width, local_heads * width_qkv)
    normed = (
        lax.all_gather(tokens, "tensor", axis=1, tiled=True).astype(jnp.float32)
        * inverse[:, None]
        * norm_gain[None, :]
    ).astype(jnp.bfloat16)
    qkv_sum = jnp.dot(normed, flat_qkv, preferred_element_type=jnp.float32)
    gate_sum = jnp.dot(normed, w_gate_out, preferred_element_type=jnp.float32)
    low_rank = jnp.dot(normed, gate_down, preferred_element_type=jnp.float32)
    projected = qkv_sum.astype(jnp.bfloat16).reshape(row_count, local_heads, width_qkv)
    gate_rounded = lax.optimization_barrier(gate_sum.astype(jnp.bfloat16))
    gate_values = gate_rounded.astype(jnp.float32).reshape(row_count, local_heads, value_width)
    logits = jnp.dot(
        low_rank, gate_up.reshape(gate_up.shape[0], local_heads * key_width), precision=EXACT_MATMUL
    )
    logits = logits.reshape(row_count, local_heads, key_width) + gate_bias[None]
    log_decay = jnp.where(valid[:, None, None], jax.nn.log_sigmoid(logits) / 16.0, 0.0)
    tail_rows = projected[row_count - taps + 1 :]
    previous = from_behind(tail_rows, "seq", 1)
    previous = jnp.where(is_start, jnp.zeros_like(previous), previous)
    extended = jnp.concatenate([previous, projected], axis=0)
    conv_sum = jnp.zeros((row_count, local_heads, width_qkv), jnp.float32)
    for offset in range(taps):
        conv_sum = conv_sum + conv_weight[offset][None] * extended[
            offset : offset + row_count
        ].astype(jnp.float32)
    activated = jax.nn.silu(conv_sum).astype(jnp.bfloat16)
    query_rows = activated[:, :, :key_width].astype(jnp.float32) * key_width ** (-0.5)
    key_rows = jnp.where(
        valid[:, None, None],
        activated[:, :, key_width : 2 * key_width],
        jnp.zeros((), jnp.bfloat16),
    )
    value_rows = activated[:, :, 2 * key_width :]

    def into_blocks(array):
        return array.reshape(row_count // STRETCH, STRETCH, local_heads, array.shape[-1])

    start_carry = (
        jnp.zeros((local_heads, key_width, value_width), jnp.float32),
        jnp.zeros((local_heads, key_width), jnp.float32),
    )
    (local_state, decay_sum), (local_out, block_starts, block_offsets, query_decayed) = lax.scan(
        block_pass,
        start_carry,
        (
            into_blocks(query_rows),
            into_blocks(key_rows),
            into_blocks(value_rows),
            into_blocks(log_decay),
        ),
    )
    decay_total = jnp.exp(decay_sum)
    span_most = 3 * lax.axis_size("seq") // 4

    def relay(turn, carry):
        received, outgoing = carry
        received = from_behind(outgoing, "seq", 1)
        received = jnp.where(is_start, jnp.zeros_like(received), received)
        return (received, decay_total[:, :, None] * received + local_state)

    incoming, _ = lax.fori_loop(0, span_most - 1, relay, (jnp.zeros_like(local_state), local_state))
    full_starts = block_starts + jnp.exp(block_offsets)[:, :, :, None] * incoming[None]
    cross_block_term = jnp.einsum(
        "bchk,bhkv->bchv",
        query_decayed,
        full_starts.astype(jnp.bfloat16),
        preferred_element_type=jnp.float32,
    )
    attended = (cross_block_term + local_out).reshape(row_count, local_heads, value_width)
    end_state = decay_total[:, :, None] * incoming + local_state
    mean_square = jnp.mean(attended * attended, axis=2, keepdims=True)
    gated = (
        attended
        * lax.rsqrt(mean_square + EPS_HEAD)
        * head_gain[None, None, :]
        * jax.nn.silu(gate_values)
    ).astype(jnp.bfloat16)
    gated = gated.reshape(row_count, local_heads * value_width)
    share = row_count // lax.axis_size("tensor")
    summed = lax.psum_scatter(
        jnp.dot(gated, w_out, preferred_element_type=jnp.float32).astype(jnp.bfloat16),
        "tensor",
        scatter_dimension=0,
        tiled=True,
    ).astype(jnp.float32)
    own_rows = lax.axis_index("tensor") * share + jnp.arange(share, dtype=jnp.int32)
    mixed = jnp.where((own_rows < live_rows)[:, None], summed, 0.0).astype(jnp.bfloat16)
    edge_rows = lax.dynamic_slice_in_dim(extended, live_rows, taps - 1, 0)
    edge_wide = edge_rows.astype(jnp.float32)

    def deliver(turn, carry):
        states_sofar, edges_sofar = carry
        root = jnp.sum(jnp.where(jnp.arange(prompts, dtype=jnp.int32) == turn, span_ends - 1, 0))
        got_state, got_edge = (
            broadcast(end_state.astype(jnp.bfloat16), "seq", root).astype(end_state.dtype),
            broadcast(edge_wide.astype(jnp.bfloat16), "seq", root).astype(edge_wide.dtype),
        )
        wanted = (request_prompt == turn)[:, None, None, None]
        return (
            jnp.where(wanted, got_state[None], states_sofar),
            jnp.where(wanted, got_edge[None], edges_sofar),
        )

    empty = (
        jnp.zeros((slot_count, local_heads, key_width, value_width), jnp.float32),
        jnp.zeros((slot_count, taps - 1, local_heads, width_qkv), jnp.float32),
    )
    owner_state, owner_wide = lax.fori_loop(0, prompts, deliver, empty)
    owner_edge = owner_wide.astype(jnp.bfloat16)
    return (mixed, owner_state, owner_edge)


def solution(mesh):
    return jax.shard_map(
        body,
        mesh=mesh,
        in_specs=(
            P("seq", "tensor"),
            P(),
            P(None, "tensor", None),
            P(None, "tensor"),
            P(),
            P(None, "tensor", None),
            P("tensor", None),
            P(None, "tensor", None),
            P(),
            P("tensor", None),
            P(),
            P(),
            P("seq"),
        ),
        out_specs=(
            P(("seq", "tensor"), None),
            P("seq", "tensor", None, None),
            P("seq", None, "tensor", None),
        ),
        check_vma=False,
    )
```

profile of v0, /device:TPU:1, one launch (start us, length us, event | category | flops | bytes accessed | tf_op | source)
XLA Modules:
  0.0 1430.1 jit_solution(8142053873680387150)
XLA Ops:
  14.6 9.3 psum.35
  24.7 22.1 %all-gather.2.cloned.1.call-done = bf16[512,2048]{1,0:T(8,128)(2,1)} async-done(((bf16[512,512]{1,0:T(8,128)(2,1)}), bf16[512,2048]{1,0:T(8,128)(2,1)}) %all-gather.2.cloned.1.call-update) | async-done | bytes 2097168 | tf_op jit(solution)/shard_map/all_gather | solution.py:88
  64.2 61.5 %while.52 = (s32[]{:T(128)}, f32[1,256,512]{2,1,0:T(8,128)S(1)}, f32[1,256]{1,0:T(1,128)S(1)}, f32[8,64,1,512]{3,1,2,0:T(8,128)}, f32[8,1,256,512]{3,2,1,0:T(8,1...) while((s32[]{:T(128)}, f32[1,256,512]{2,1,0:T(8,128)S(1)}, ...), condition=%wide.region_9.10_spmd.clone, body=%wide.region_7.9_spmd.clone.sunk | while | flops 27890436 | bytes 12177578 | solution.py:128
  126.6 613.5 %while.51 = (s32[]{:T(128)}, f32[1,256,512]{2,1,0:T(8,128)}, f32[1,256,512]{2,1,0:T(8,128)}, pred[]{:T(512)}, f32[1,256]{1,0:T(1,128)S(1)}, /*index=5*/f32[1,256,512]{2,1,0:T(8,128)S(1)}, s32[]{:T(128)}) while((s32[]{:T(128)}, f32[1,256,512]{2,1,0:T(8,128)}, f32[1,256,512]{2,1,0:T(8,128)}, pred[]{:T(512)}, f32[1,256]{1,0:T(1,128)S(1)}, ...), condition=%wide.region_11.12_spmd, body=%wide.region_10.11_spmd.sunk | while | flops 393218 | bytes 4195446 | solution.py:147
  128.6 6.4 collective-permute-done
  140.4 6.4 collective-permute-done
  152.2 6.4 collective-permute-done
  164.0 6.4 collective-permute-done
  175.8 6.4 collective-permute-done
  187.6 6.4 collective-permute-done
  199.4 6.4 collective-permute-done
  211.2 6.4 collective-permute-done
  223.0 6.4 collective-permute-done
  234.8 6.4 collective-permute-done
  246.7 6.4 collective-permute-done
  258.5 6.4 collective-permute-done
  270.3 6.4 collective-permute-done
  282.1 6.4 collective-permute-done
  293.9 6.4 collective-permute-done
  305.7 6.4 collective-permute-done
  317.5 6.4 collective-permute-done
  329.3 6.4 collective-permute-done
  342.9 6.4 collective-permute-done
  356.9 6.4 collective-permute-done
  364.4 6.4 collective-permute-start
  370.8 6.4 collective-permute-done
  378.3 6.4 collective-permute-start
  384.7 6.4 collective-permute-done
  398.6 6.4 collective-permute-done
  412.5 6.4 collective-permute-done
  420.0 6.4 collective-permute-start
  426.4 6.4 collective-permute-done
  440.3 6.4 collective-permute-done
  454.2 6.4 collective-permute-done
  468.2 6.4 collective-permute-done
  475.7 6.4 collective-permute-start
  482.1 6.4 collective-permute-done
  496.0 6.4 collective-permute-done
  509.9 6.4 collective-permute-done
  523.8 6.4 collective-permute-done
  531.3 6.4 collective-permute-start
  537.7 6.4 collective-permute-done
  551.6 6.4 collective-permute-done
  565.5 6.4 collective-permute-done
  579.5 6.4 collective-permute-done
  593.4 6.4 collective-permute-done
  607.3 6.4 collective-permute-done
  621.2 6.4 collective-permute-done
  635.1 6.4 collective-permute-done
  649.0 6.4 collective-permute-done
  662.9 6.4 collective-permute-done
  676.8 6.4 collective-permute-done
  690.8 6.4 collective-permute-done
  704.7 6.4 collective-permute-done
  718.6 6.4 collective-permute-done
  732.5 6.4 collective-permute-done
  748.9 640.3 %while.53 = (s32[]{:T(128)}, f32[2,1,256,512]{3,2,1,0:T(8,128)S(1)}, bf16[2,3,1,1024]{3,2,1,0:T(2,128)(2,1)S(1)}, s32[2]{0:T(128)S(1)}, s32[3]{0:T(128)S(1)}, /*...) while((s32[]{:T(128)}, ...), condition=%wide.region_18.19_spmd.clone, body=%wide.region_14.18_spmd.clone.sunk | while | flops 935956 | bytes 5560569 | solution.py:194
  750.9 160.4 %psum.41 = bf16[3,1024]{1,0:T(4,128)(2,1)S(1)} all-reduce(bf16[3,1024]{1,0:T(4,128)(2,1)S(1)} %select_bitcast_fusion.5), channel_id=1, replica_groups=mesh['seq'=64,'tensor'=4] {'seq'}, use_global_device_ids=true, to_apply=%region_17.17 | all-reduce | flops 3072 | bytes 12288 | tf_op jit(solution)/shard_map/while/body/eval_jaxpr/psum | solution.py:22
  911.5 114.8 %all-reduce.2.cloned.1.call-done = bf16[256,512]{1,0:T(8,128)(2,1)} async-done(((bf16[256,512]{1,0:T(8,128)(2,1)}), bf16[256,512]{1,0:T(8,128)(2,1)}) %all-reduce.2.cloned.1.call-update) | async-done | bytes 262160 | tf_op jit(solution)/shard_map/while/body/eval_jaxpr/psum | solution.py:22
  1029.7 124.7 %psum.41 = bf16[3,1024]{1,0:T(4,128)(2,1)S(1)} all-reduce(bf16[3,1024]{1,0:T(4,128)(2,1)S(1)} %select_bitcast_fusion.5), channel_id=1, replica_groups=mesh['seq'=64,'tensor'=4] {'seq'}, use_global_device_ids=true, to_apply=%region_17.17 | all-reduce | flops 3072 | bytes 12288 | tf_op jit(solution)/shard_map/while/body/eval_jaxpr/psum | solution.py:22
  1154.5 52.8 %all-reduce.2.cloned.1.call-done = bf16[256,512]{1,0:T(8,128)(2,1)} async-done(((bf16[256,512]{1,0:T(8,128)(2,1)}), bf16[256,512]{1,0:T(8,128)(2,1)}) %all-reduce.2.cloned.1.call-update) | async-done | bytes 262160 | tf_op jit(solution)/shard_map/while/body/eval_jaxpr/psum | solution.py:22
  1210.7 124.6 %psum.41 = bf16[3,1024]{1,0:T(4,128)(2,1)S(1)} all-reduce(bf16[3,1024]{1,0:T(4,128)(2,1)S(1)} %select_bitcast_fusion.5), channel_id=1, replica_groups=mesh['seq'=64,'tensor'=4] {'seq'}, use_global_device_ids=true, to_apply=%region_17.17 | all-reduce | flops 3072 | bytes 12288 | tf_op jit(solution)/shard_map/while/body/eval_jaxpr/psum | solution.py:22
  1335.4 52.5 %all-reduce.2.cloned.1.call-done = bf16[256,512]{1,0:T(8,128)(2,1)} async-done(((bf16[256,512]{1,0:T(8,128)(2,1)}), bf16[256,512]{1,0:T(8,128)(2,1)}) %all-reduce.2.cloned.1.call-update) | async-done | bytes 262160 | tf_op jit(solution)/shard_map/while/body/eval_jaxpr/psum | solution.py:22
  1390.4 31.2 %reduce-scatter.2.cloned.1.call-done = bf16[128,2048]{1,0:T(8,128)(2,1)} async-done(((bf16[512,2048]{1,0:T(8,128)(2,1)}), bf16[128,2048]{1,0:T(8,128)(2,1)}) %reduce-scatter.2.cloned.1.call-update) | async-done | bytes 524304 | tf_op jit(solution)/shard_map/reduce_scatter | solution.py:166
  (338 shorter events, 385.0 us)
Async XLA Ops:
  7.2 739.1 %copy-start = (bf16[512,2048]{1,0:T(8,128)(2,1)S(1)}, bf16[512,2048]{1,0:T(8,128)(2,1)}, u32[]{:S(2)}) copy-start(bf16[512,2048]{1,0:T(8,128)(2,1)} %param.28) | copy-start | bytes 6291460
  7.2 39.6 %all-gather.2.cloned.1.call-start = ((), (), s32[]{:S(2)}) async-start(), calls=%async_computation.1 | async-start | bytes 2621440 | tf_op jit(solution)/shard_map/all_gather | solution.py:88
  24.7 31.7 %copy-start.13 = (f32[2048]{0:T(1024)S(1)}, f32[2048]{0:T(1024)}, u32[]{:S(2)}) copy-start(f32[2048]{0:T(1024)} %param.20) | copy-start | bytes 24580
  46.8 9.6 copy-start.9
  46.8 9.6 copy-start.10
  52.1 8.8 copy-start.3
  52.2 6.3 copy-start.11
  52.2 8.7 collective-permute-start.1
  126.5 613.5 %copy-start.7 = (bf16[8,64,1,256]{3,1,2,0:T(8,128)(2,1)S(1)}, bf16[8,64,1,256]{3,1,2,0:T(8,128)(2,1)}, u32[]{:S(2)}) copy-start(bf16[8,64,1,256]{3,1,2,0:T(8,128)(2,1)} %get-tuple-element.282) | copy-start | bytes 786436
  126.6 8.5 collective-permute-start
  136.1 10.7 collective-permute-start
  148.0 10.7 collective-permute-start
  159.8 10.7 collective-permute-start
  171.6 10.7 collective-permute-start
  183.4 10.7 collective-permute-start
  195.2 10.7 collective-permute-start
  207.0 10.7 collective-permute-start
  218.8 10.7 collective-permute-start
  230.6 10.7 collective-permute-start
  242.4 10.7 collective-permute-start
  254.2 10.7 collective-permute-start
  266.0 10.7 collective-permute-start
  277.8 10.7 collective-permute-start
  289.6 10.7 collective-permute-start
  301.4 10.7 collective-permute-start
  313.2 10.7 collective-permute-start
  325.0 10.7 collective-permute-start
  336.8 12.6 collective-permute-start
  350.5 12.8 collective-permute-start
  364.4 12.8 collective-permute-start
  378.3 12.8 collective-permute-start
  392.2 12.8 collective-permute-start
  406.1 12.8 collective-permute-start
  420.0 12.8 collective-permute-start
  433.9 12.8 collective-permute-start
  447.9 12.8 collective-permute-start
  461.8 12.8 collective-permute-start
  475.7 12.8 collective-permute-start
  489.6 12.8 collective-permute-start
  503.5 12.8 collective-permute-start
  517.4 12.8 collective-permute-start
  531.3 12.8 collective-permute-start
  545.2 12.8 collective-permute-start
  559.2 12.8 collective-permute-start
  573.1 12.8 collective-permute-start
  587.0 12.8 collective-permute-start
  600.9 12.8 collective-permute-start
  614.8 12.8 collective-permute-start
  628.7 12.8 collective-permute-start
  642.6 12.8 collective-permute-start
  656.5 12.8 collective-permute-start
  670.4 12.8 collective-permute-start
  684.4 12.8 collective-permute-start
  698.3 12.8 collective-permute-start
  712.2 12.8 collective-permute-start
  726.1 12.8 collective-permute-start
  740.0 4.5 copy-start.5
  746.2 2.6 copy-start.1
  746.2 2.6 copy-start.15
  748.9 277.4 %all-reduce.2.cloned.1.call-start = ((), (), s32[]{:S(2)}) async-start(), calls=%async_computation.3 | async-start | bytes 524288 | tf_op jit(solution)/shard_map/while/body/eval_jaxpr/psum | solution.py:22
  1027.6 179.7 %all-reduce.2.cloned.1.call-start = ((), (), s32[]{:S(2)}) async-start(), calls=%async_computation.3 | async-start | bytes 524288 | tf_op jit(solution)/shard_map/while/body/eval_jaxpr/psum | solution.py:22
  1208.6 179.3 %all-reduce.2.cloned.1.call-start = ((), (), s32[]{:S(2)}) async-start(), calls=%async_computation.3 | async-start | bytes 524288 | tf_op jit(solution)/shard_map/while/body/eval_jaxpr/psum | solution.py:22
  1389.2 34.4 %copy-start.2 = (f32[2,1,256,512]{3,2,1,0:T(8,128)}, f32[2,1,256,512]{3,2,1,0:T(8,128)S(1)}, u32[]{:S(2)}) copy-start(f32[2,1,256,512]{3,2,1,0:T(8,128)S(1)} %get-tuple-element.275) | copy-start | bytes 3145732
  1389.2 32.4 %reduce-scatter.2.cloned.1.call-start = ((), (), s32[]{:S(2)}) async-start(), calls=%async_computation.2 | async-start | bytes 2621440 | tf_op jit(solution)/shard_map/reduce_scatter | solution.py:166
  (5 other events, 5.3 us)
Sparse Core Ops, SparseCore 0:
  9.8 36.9 all-gather.1
  753.7 272.5 all-reduce.1
  1032.5 174.7 all-reduce.1
  1213.1 174.7 all-reduce.1
  1392.3 29.2 reduce-scatter.1
where the time goes:
time: 1430 us
  waiting for transfers between devices  576 us (40%)
  blocking collectives  419 us (29%)
  starting transfers between devices  264 us (18%)
  other arithmetic  105 us (7%)
  matrix products  25.5 us (2%)
  local copies, waits for them, and re-layouts  21.6 us (2%)
  between operations  15.9 us (1%)
    psum x3, blocking collectives, broadcast(): return lax.psum(block, axis)  410 us
    ppermute x48, waiting for transfers between devices, from_behind(): return lax.ppermute(array, axis, pairs)  302 us
    ppermute x48, starting transfers between devices, from_behind(): return lax.ppermute(array, axis, pairs)  264 us
    psum x3, waiting for transfers between devices, broadcast(): return lax.psum(block, axis)  220 us
    add x47, other arithmetic, relay(): return (received, decay_total[:, :, None] * received + local_state)  51.8 us
    reduce_scatter x1, waiting for transfers between devices, body(): lax.psum_scatter(jnp.dot(gated, w_out, preferred_element_type=jnp.float32...  31.2 us
  transfers between devices with their start and end apart: 53, of which 52 were waited for; matrix products, arithmetic and copies ran while one was open for 1% of the time, Pallas kernels for 0%

commit v1 on v0

--- a/solution.py
+++ b/solution.py
@@ -1,6 +1,10 @@
+import functools
+
 import jax
 import jax.numpy as jnp
 from jax import lax
+from jax.experimental import pallas as pl
+from jax.experimental.pallas import tpu as pltpu
 from jax.sharding import PartitionSpec as P
 
 STRETCH = 64
@@ -9,6 +13,7 @@
 EPS_IN = 1e-06
 EPS_HEAD = 1e-05
 EXACT_MATMUL = lax.Precision.HIGHEST
+MESH = pl.DeviceIdType.MESH
 
 
 def from_behind(array, axis, by):
@@ -17,9 +22,203 @@
     return lax.ppermute(array, axis, pairs)
 
 
-def broadcast(block, axis, source):
-    block = jnp.where(lax.axis_index(axis) == source, block, jnp.zeros_like(block))
-    return lax.psum(block, axis)
+def handoff_kernel(
+    n,
+    rows,
+    start_ref,
+    end_ref,
+    state_ref,
+    message_ref,
+    incoming_ref,
+    owned_ref,
+    parts,
+    messages,
+    back,
+    handed,
+    incoming,
+    owned,
+    send_part,
+    recv_part,
+    send_message,
+    recv_message,
+    send_back,
+    recv_back,
+    send_handed,
+    recv_handed,
+):
+    me = lax.axis_index("seq")
+    lane_blocks = state_ref.shape[1] // 128
+
+    def block_of(index):
+        return (
+            pl.ds(pl.multiple_of((index // lane_blocks) * rows, rows), rows),
+            pl.ds(pl.multiple_of((index % lane_blocks) * 128, 128), 128),
+        )
+
+    barrier = pltpu.get_barrier_semaphore()
+
+    def greet(step, _):
+        peer = lax.rem(me + step, n)
+        pl.semaphore_signal(barrier, inc=1, device_id={"seq": peer}, device_id_type=MESH)
+        return 0
+
+    lax.fori_loop(1, n, greet, 0)
+    pl.semaphore_wait(barrier, n - 1)
+
+    my_block = block_of(me)
+
+    def message_to(peer):
+        return pltpu.make_async_remote_copy(
+            src_ref=message_ref,
+            dst_ref=messages.at[me],
+            send_sem=send_message.at[peer],
+            recv_sem=recv_message.at[me],
+            device_id={"seq": peer},
+            device_id_type=MESH,
+        )
+
+    def part_to(peer):
+        return pltpu.make_async_remote_copy(
+            src_ref=state_ref.at[block_of(peer)],
+            dst_ref=parts.at[me],
+            send_sem=send_part.at[peer],
+            recv_sem=recv_part.at[me],
+            device_id={"seq": peer},
+            device_id_type=MESH,
+        )
+
+    def back_to(peer):
+        return pltpu.make_async_remote_copy(
+            src_ref=back.at[peer],
+            dst_ref=incoming.at[my_block],
+            send_sem=send_back.at[peer],
+            recv_sem=recv_back.at[me],
+            device_id={"seq": peer},
+            device_id_type=MESH,
+        )
+
+    def handed_to(peer):
+        return pltpu.make_async_remote_copy(
+            src_ref=handed.at[peer],
+            dst_ref=owned.at[(slice(None),) + my_block],
+            send_sem=send_handed.at[peer],
+            recv_sem=recv_handed.at[me],
+            device_id={"seq": peer},
+            device_id_type=MESH,
+        )
+
+    def send_first(step, _):
+        peer = lax.rem(me + step, n)
+        message_to(peer).start()
+        part_to(peer).start()
+        return 0
+
+    lax.fori_loop(1, n, send_first, 0)
+    parts[me] = state_ref[my_block]
+    messages[me] = message_ref[...]
+
+    def arrived(make, ref_of, sem):
+        def wait(step, _):
+            peer = lax.rem(me + step, n)
+            ref = ref_of(peer)
+            pltpu.make_async_copy(ref, ref, sem.at[peer]).wait()
+            return 0
+
+        lax.fori_loop(1, n, wait, 0)
+
+    arrived(None, lambda peer: messages.at[peer], recv_message)
+    arrived(None, lambda peer: parts.at[peer], recv_part)
+
+    key_row = (me // lane_blocks) * rows
+    lanes = lax.broadcasted_iota(jnp.int32, (rows, 128), 1)
+    sublanes = lax.broadcasted_iota(jnp.int32, (rows, 128), 0)
+    offset = key_row % 128 + sublanes
+    key_lanes = pl.ds(pl.multiple_of((key_row // 128) * 128, 128), 128)
+    zero = jnp.zeros((rows, 128), jnp.float32)
+
+    def scan(index, carry):
+        running, finals = carry
+        running = jnp.where(start_ref[index] == 1, zero, running)
+        back[index] = running.astype(jnp.bfloat16)
+
+        @pl.when(index != me)
+        def _():
+            back_to(index).start()
+
+        row = messages[index, :, key_lanes]
+        decay = jnp.sum(jnp.where(lanes == offset, row, 0.0), axis=1, keepdims=True)
+        running = decay * running + parts[index].astype(jnp.float32)
+        ended = end_ref[index]
+        finals = tuple(jnp.where(ended == p, running, f) for p, f in enumerate(finals))
+        return running, finals
+
+    _, finals = lax.fori_loop(0, n, scan, (zero, (zero, zero, zero)))
+
+    def hand(step, _):
+        peer = lax.rem(me + step, n)
+        for slot in range(2):
+            wanted = messages[peer, :, pl.ds(256 + 128 * slot, 128)]
+            picked = zero
+            for p, final in enumerate(finals):
+                picked = jnp.where(wanted == float(p), final, picked)
+            handed[peer, slot] = picked.astype(jnp.bfloat16)
+
+        @pl.when(step > 0)
+        def _():
+            handed_to(peer).start()
+
+        return 0
+
+    lax.fori_loop(0, n, hand, 0)
+    incoming[my_block] = back[me]
+    owned[(slice(None),) + my_block] = handed[me]
+
+    arrived(None, lambda peer: incoming.at[block_of(peer)], recv_back)
+    incoming_ref[...] = incoming[...]
+    arrived(None, lambda peer: owned.at[(slice(None),) + block_of(peer)], recv_handed)
+    owned_ref[...] = owned[...].astype(jnp.float32)
+
+    def drain(step, _):
+        peer = lax.rem(me + step, n)
+        message_to(peer).wait_send()
+        part_to(peer).wait_send()
+        back_to(peer).wait_send()
+        handed_to(peer).wait_send()
+        return 0
+
+    lax.fori_loop(1, n, drain, 0)
+
+
+def handoff(state, decay, wanted, starts_here, ends_here):
+    n = lax.axis_size("seq")
+    keys, values = state.shape
+    rows = keys * (values // 128) // n
+    message = jnp.concatenate(
+        [decay[None], jnp.broadcast_to(wanted.astype(jnp.float32)[:, None], (2, 128)).reshape(1, 256)],
+        axis=1,
+    )
+    vmem = pl.BlockSpec(memory_space=pltpu.VMEM)
+    smem = pl.BlockSpec(memory_space=pltpu.SMEM)
+    return pl.pallas_call(
+        functools.partial(handoff_kernel, n, rows),
+        out_shape=(
+            jax.ShapeDtypeStruct((keys, values), jnp.bfloat16),
+            jax.ShapeDtypeStruct((2, keys, values), jnp.float32),
+        ),
+        in_specs=[smem, smem, vmem, vmem],
+        out_specs=(vmem, vmem),
+        scratch_shapes=[
+            pltpu.VMEM((n, rows, 128), jnp.bfloat16),
+            pltpu.VMEM((n, 1, 512), jnp.float32),
+            pltpu.VMEM((n, rows, 128), jnp.bfloat16),
+            pltpu.VMEM((n, 2, rows, 128), jnp.bfloat16),
+            pltpu.VMEM((keys, values), jnp.bfloat16),
+            pltpu.VMEM((2, keys, values), jnp.bfloat16),
+        ]
+        + [pltpu.SemaphoreType.DMA((n,))] * 8,
+        compiler_params=pltpu.CompilerParams(collective_id=0, has_side_effects=True),
+        name="state_handoff",
+    )(starts_here, ends_here, state.astype(jnp.bfloat16), message)
 
 
 def block_pass(carry, pieces):
@@ -135,16 +334,21 @@
             into_blocks(log_decay),
         ),
     )
-    decay_total = jnp.exp(decay_sum)
-    span_most = 3 * lax.axis_size("seq") // 4
-
-    def relay(turn, carry):
-        received, outgoing = carry
-        received = from_behind(outgoing, "seq", 1)
-        received = jnp.where(is_start, jnp.zeros_like(received), received)
-        return (received, decay_total[:, :, None] * received + local_state)
-
-    incoming, _ = lax.fori_loop(0, span_most - 1, relay, (jnp.zeros_like(local_state), local_state))
+    devices = jnp.arange(lax.axis_size("seq"), dtype=jnp.int32)
+    starts_here = jnp.any(devices[:, None] == starts[None, :], axis=1).astype(jnp.int32)
+    ends_here = jnp.sum(
+        jnp.where(
+            devices[:, None] == span_ends[None, :] - 1,
+            jnp.arange(prompts, dtype=jnp.int32)[None, :] + 1,
+            0,
+        ),
+        axis=1,
+    ) - 1
+    incoming, owner_state = handoff(
+        local_state[0], jnp.exp(decay_sum)[0], request_prompt, starts_here, ends_here
+    )
+    incoming = incoming.astype(jnp.float32)[None]
+    owner_state = owner_state[:, None]
     full_starts = block_starts + jnp.exp(block_offsets)[:, :, :, None] * incoming[None]
     cross_block_term = jnp.einsum(
         "bchk,bhkv->bchv",
@@ -153,7 +357,6 @@
         preferred_element_type=jnp.float32,
     )
     attended = (cross_block_term + local_out).reshape(row_count, local_heads, value_width)
-    end_state = decay_total[:, :, None] * incoming + local_state
     mean_square = jnp.mean(attended * attended, axis=2, keepdims=True)
     gated = (
         attended
@@ -172,27 +375,11 @@
     own_rows = lax.axis_index("tensor") * share + jnp.arange(share, dtype=jnp.int32)
     mixed = jnp.where((own_rows < live_rows)[:, None], summed, 0.0).astype(jnp.bfloat16)
     edge_rows = lax.dynamic_slice_in_dim(extended, live_rows, taps - 1, 0)
-    edge_wide = edge_rows.astype(jnp.float32)
-
-    def deliver(turn, carry):
-        states_sofar, edges_sofar = carry
-        root = jnp.sum(jnp.where(jnp.arange(prompts, dtype=jnp.int32) == turn, span_ends - 1, 0))
-        got_state, got_edge = (
-            broadcast(end_state.astype(jnp.bfloat16), "seq", root).astype(end_state.dtype),
-            broadcast(edge_wide.astype(jnp.bfloat16), "seq", root).astype(edge_wide.dtype),
-        )
-        wanted = (request_prompt == turn)[:, None, None, None]
-        return (
-            jnp.where(wanted, got_state[None], states_sofar),
-            jnp.where(wanted, got_edge[None], edges_sofar),
-        )
-
-    empty = (
-        jnp.zeros((slot_count, local_heads, key_width, value_width), jnp.float32),
-        jnp.zeros((slot_count, taps - 1, local_heads, width_qkv), jnp.float32),
-    )
-    owner_state, owner_wide = lax.fori_loop(0, prompts, deliver, empty)
-    owner_edge = owner_wide.astype(jnp.bfloat16)
+    ending = (is_last & picked)[:, None, None, None]
+    edges = lax.psum(jnp.where(ending, edge_rows[None], jnp.zeros((), jnp.bfloat16)), "seq")
+    owner_edge = jnp.zeros((slot_count,) + edge_rows.shape, jnp.bfloat16)
+    for p in range(prompts):
+        owner_edge = jnp.where((request_prompt == p)[:, None, None, None], edges[p][None], owner_edge)
     return (mixed, owner_state, owner_edge)
 
 

time: 1430 us -> 443 us (0.31)
  waiting for transfers between devices: 576 us -> 20.8 us
  starting transfers between devices: 264 us -> 4.36 us
  blocking collectives: 419 us -> 255 us
  other arithmetic: 105 us -> 49.9 us
  Pallas kernels: 0 us -> 50.4 us
    ppermute x48 -> x1, waiting for transfers between devices: 302 us -> 0.01 us  [from_behind(): return lax.ppermute(array, axis, pairs)]
    ppermute x48 -> x1, starting transfers between devices: 264 us -> 4.29 us  [from_behind(): return lax.ppermute(array, axis, pairs)]
    psum x3 -> x0, waiting for transfers between devices: 220 us -> none  [broadcast(): return lax.psum(block, axis)]
    psum x3 -> x1, blocking collectives: 410 us -> 245 us  [body(): lax.psum(jnp.where(ending, edge_rows[None], jnp.zeros((), jnp.bfloat16)),...]
    add x47 -> x1, other arithmetic: 51.8 us -> 0.01 us  [body(): jnp.arange(prompts, dtype=jnp.int32)[None, :] + 1]
    pallas_call x0 -> x1, Pallas kernels: none -> 50.4 us  [handoff(): pl.pallas_call(functools.partial(handoff_kernel, n, rows), out_shape=(jax...]
    reduce_scatter x1, waiting for transfers between devices: 31.2 us -> 0.01 us  [body(): lax.psum_scatter(jnp.dot(gated, w_out, preferred_element_type=jnp.float32...]
  transfers between devices with their start and end apart: 53 -> 3, of which waited for: 52 -> 1; matrix products, arithmetic and copies ran while one was open for 1% -> 3% of each run, Pallas kernels for 0% -> 0%
where the time goes in v1:
time: 443 us; the launch traced here: 438 us
  blocking collectives  255 us (58%)
  Pallas kernels  50.4 us (11%)
  other arithmetic  49.9 us (11%)
  matrix products  24.6 us (6%)
  waiting for transfers between devices  20.8 us (5%)
  local copies, waits for them, and re-layouts  16.7 us (4%)
  between operations  16.2 us (4%)
    psum x1, blocking collectives, body(): lax.psum(jnp.where(ending, edge_rows[None], jnp.zeros((), jnp.bfloat16)),...  245 us
    pallas_call x1, Pallas kernels, handoff(): pl.pallas_call(functools.partial(handoff_kernel, n, rows), out_shape=(jax...  50.4 us
    all_gather x1, waiting for transfers between devices, body(): lax.all_gather(tokens, 'tensor', axis=1, tiled=True).astype(jnp.float32)  20.1 us
    while x8, other arithmetic  19.3 us
    psum x1, blocking collectives, body(): squares = lax.psum(jnp.sum(value_entries * value_entries, axis=1), 'tensor')  9.29 us
  transfers between devices with their start and end apart: 3, of which 1 were waited for; matrix products, arithmetic and copies ran while one was open for 3% of the time, Pallas kernels for 0%

profile of v1, /device:TPU:1, one launch (start us, length us, event | category | flops | bytes accessed | tf_op | source)
XLA Modules:
  0.0 438.5 jit_solution(10900917906140690314)
XLA Ops:
  7.2 0.7 all-gather.2.cloned.1.call-update
  8.0 0.8 reduce-window.7
  8.9 0.7 convert_element_type.110
  9.5 0.7 fusion.53
  10.2 2.0 bitcast_add_fusion.2
  14.8 1.2 multiply_reduce_fusion.1
  16.0 9.3 %psum.14 = f32[512]{0:T(512)S(1)} all-reduce(f32[512]{0:T(512)S(1)} %multiply_reduce_fusion.1), channel_id=1, replica_groups=mesh['seq'=64,'tensor'=4] {'tensor'}, use_global_device_ids=true, to_apply=%region_6.7 | all-reduce | flops 512 | bytes 4096 | tf_op jit(solution)/shard_map/psum | solution.py:283
  25.9 0.8 fusion.55
  26.7 20.1 %all-gather.2.cloned.1.call-done = bf16[512,2048]{1,0:T(8,128)(2,1)} async-done(((bf16[512,512]{1,0:T(8,128)(2,1)}), bf16[512,2048]{1,0:T(8,128)(2,1)}) %all-gather.2.cloned.1.call-update) | async-done | bytes 2097168 | tf_op jit(solution)/shard_map/all_gather | solution.py:287
  46.8 5.4 %fusion.25 = bf16[512,1024]{1,0:T(8,128)(2,1)S(1)} fusion(bf16[2048,1,1024]{2,0,1:T(8,128)(2,1)} %param.17, bf16[512,2048]{1,0:T(8,128)(2,1)} %all-gather.2.cloned.1.call-done, f32[2048]{0:T(1024)} %param.16, f32[512]{0:T(512)S(1)} %add_rsqrt_fusion.1), kind=kOutput, calls=%fused_computation.55 | convolution fusion | flops 2152202240 | bytes 7350272 | tf_op jit(solution)/shard_map/dot_general | solution.py:291
  52.2 4.3 collective-permute-start
  56.5 0.7 fusion.54
  57.2 2.1 convolution_convert_fusion.1
  59.3 1.7 fusion.46
  61.1 1.5 multiply_convert_fusion.1
  62.7 0.9 convert_multiply_fusion.1
  63.6 55.8 %while.21 = (s32[]{:T(128)}, f32[1,256,512]{2,1,0:T(8,128)S(1)}, f32[1,256]{1,0:T(1,128)S(1)}, f32[8,64,1,512]{3,1,2,0:T(8,128)}, f32[8,1,256,512]{3,2,1,0:T(8,1...) while((s32[]{:T(128)}, f32[1,256,512]{2,1,0:T(8,128)S(1)}, ...), condition=%wide.region_9.10_spmd.clone, body=%wide.region_7.9_spmd.clone.sunk | while | flops 27890436 | bytes 12177578 | solution.py:327
  63.7 0.9 constant_dynamic-slice_fusion.5
  66.1 2.4 fusion.75
  68.6 0.8 fusion.76
  69.5 0.8 bitcast_dynamic-update-slice_fusion.2
  70.7 0.9 constant_dynamic-slice_fusion.5
  71.9 0.6 copy_dynamic-update-slice_fusion.2
  73.1 2.4 fusion.75
  75.6 0.8 fusion.76
  76.4 0.8 bitcast_dynamic-update-slice_fusion.2
  77.7 0.9 constant_dynamic-slice_fusion.5
  80.1 2.4 fusion.75
  82.6 0.8 fusion.76
  83.4 0.9 bitcast_dynamic-update-slice_fusion.2
  84.6 0.9 constant_dynamic-slice_fusion.5
  85.9 0.6 copy_dynamic-update-slice_fusion.2
  87.1 2.4 fusion.75
  89.6 0.8 fusion.76
  90.4 0.8 bitcast_dynamic-update-slice_fusion.2
  91.6 0.9 constant_dynamic-slice_fusion.5
  94.0 2.4 fusion.75
  96.5 0.8 fusion.76
  97.4 0.8 bitcast_dynamic-update-slice_fusion.2
  98.6 0.9 constant_dynamic-slice_fusion.5
  99.8 0.6 copy_dynamic-update-slice_fusion.2
  101.0 2.4 fusion.75
  103.5 0.8 fusion.76
  104.3 0.8 bitcast_dynamic-update-slice_fusion.2
  105.6 0.9 constant_dynamic-slice_fusion.5
  108.0 2.4 fusion.75
  110.5 0.8 fusion.76
  111.3 0.8 bitcast_dynamic-update-slice_fusion.2
  112.5 0.9 constant_dynamic-slice_fusion.5
  113.7 0.6 copy_dynamic-update-slice_fusion.2
  114.9 2.4 fusion.75
  117.4 0.8 fusion.76
  118.3 0.8 bitcast_dynamic-update-slice_fusion.2
  119.4 0.7 convert_bitcast_fusion.state_ref
  120.8 50.4 %state_handoff.1 = (bf16[256,512]{1,0:T(8,128)(2,1)}, f32[2,256,512]{2,1,0:T(8,128)}) custom-call(s32[64]{0:T(128)} %convert_element_type.107.start_ref, s32[64]{0:T(128)} %broadcast_add_fusion.end_ref, bf16[256,512]{1,0:T(8,128)(2,1)} %convert_bitcast_fusion.state_ref, f32[1,512]{1,0:T(1,128)} %pad_maximum_fusion.message_ref), custom_call_target="tpu_custom_call" | custom-call | tf_op jit(solution)/shard_map/state_handoff/pallas_call | solution.py:202
  171.2 1.0 convert_element_type.111
  172.3 3.5 multiply_reduce_fusion
  175.9 1.4 fusion.43
  177.3 2.6 convolution_convert_fusion
  180.0 0.8 broadcast_and_fusion
  181.3 245.4 %psum.15 = bf16[3,3,1,1024]{3,1,2,0:T(4,128)(2,1)S(1)} all-reduce(bf16[3,3,1,1024]{3,1,2,0:T(4,128)(2,1)S(1)} %broadcast_select_fusion.2), channel_id=1, replica_groups=mesh['seq'=64,'tensor'=4] {'seq'}, use_global_device_ids=true, to_apply=%region_14.15 | all-reduce | flops 9216 | bytes 36864 | tf_op jit(solution)/shard_map/psum | solution.py:379
  426.7 0.7 broadcast_select_fusion.3
  427.4 2.0 select_convert_fusion.2
  429.4 2.3 copy.124
  (164 shorter events, 15.8 us)
Async XLA Ops:
  7.2 170.1 %copy-start = (bf16[512,2048]{1,0:T(8,128)(2,1)S(1)}, bf16[512,2048]{1,0:T(8,128)(2,1)}, u32[]{:S(2)}) copy-start(bf16[512,2048]{1,0:T(8,128)(2,1)} %param.24) | copy-start | bytes 6291460
  7.2 39.6 %all-gather.2.cloned.1.call-start = ((), (), s32[]{:S(2)}) async-start(), calls=%async_computation.1 | async-start | bytes 2621440 | tf_op jit(solution)/shard_map/all_gather | solution.py:287
  7.9 419.5 %reduce-scatter.2.cloned.1.call-start = ((), (), s32[]{:S(2)}) async-start(), calls=%async_computation.2 | async-start | bytes 2621440 | tf_op jit(solution)/shard_map/reduce_scatter | solution.py:369
  26.7 29.8 %copy-start.7 = (bf16[2048,16]{0,1:T(8,128)(2,1)S(1)}, bf16[2048,16]{0,1:T(8,128)(2,1)}, u32[]{:S(2)}) copy-start(bf16[2048,16]{0,1:T(8,128)(2,1)} %param.19) | copy-start | bytes 196612
  26.7 29.8 %copy-start.9 = (f32[2048]{0:T(1024)S(1)}, f32[2048]{0:T(1024)}, u32[]{:S(2)}) copy-start(f32[2048]{0:T(1024)} %param.16) | copy-start | bytes 24580
  46.8 9.7 %copy-start.6 = (bf16[512,2048]{1,0:T(8,128)(2,1)S(1)}, bf16[512,2048]{1,0:T(8,128)(2,1)}, u32[]{:S(2)}) copy-start(bf16[512,2048]{1,0:T(8,128)(2,1)} %all-gather.2.cloned.1.call-done) | copy-start | bytes 6291460
  52.1 8.9 %copy-start.1 = (bf16[512,1024]{1,0:T(8,128)(2,1)}, bf16[512,1024]{1,0:T(8,128)(2,1)S(1)}, u32[]{:S(2)}) copy-start(bf16[512,1024]{1,0:T(8,128)(2,1)S(1)} %fusion.25) | copy-start | bytes 3145732
  52.1 5.1 %copy-start.5 = (bf16[2048,512]{1,0:T(8,128)(2,1)S(1)}, bf16[2048,512]{1,0:T(8,128)(2,1)}, u32[]{:S(2)}) copy-start(bf16[2048,512]{1,0:T(8,128)(2,1)} %param.18) | copy-start | bytes 6291460
  52.2 8.9 %collective-permute-start = (bf16[3,1,1024]{2,0,1:T(4,128)(2,1)S(1)}, bf16[3,1,1024]{2,0,1:T(4,128)(2,1)S(1)}, u32[]{:S(2)}, u32[]{:S(2)}) collective-permute-start(bf16[3,1,1024]{2,0,1:T(4,128)(2,1)S(1)} %slice_bitcast_fusion.3), channel_id=1, source_target_pairs={{0,4},{4,8},{8,12},{12,16},{16,20},{20,24},{24,28},{28,32},{32,36}... | collective-permute-start | bytes 18440 | tf_op jit(solution)/shard_map/ppermute | solution.py:22
  57.2 2.1 copy-start.8
  57.2 2.1 copy-start.10
  172.3 3.6 copy-start.3
  179.9 0.8 copy-start.4
  179.9 1.2 copy-start.2
Sparse Core Ops, SparseCore 0:
  9.8 36.9 all-gather.1
  180.1 29.5 reduce-scatter.1

commit v2 on v1

--- a/solution.py
+++ b/solution.py
@@ -24,13 +24,16 @@
 
 def handoff_kernel(
     n,
+    group,
     rows,
     start_ref,
     end_ref,
     state_ref,
     message_ref,
+    edge_ref,
     incoming_ref,
     owned_ref,
+    owned_edge_ref,
     parts,
     messages,
     back,
@@ -45,6 +48,13 @@
     recv_back,
     send_handed,
     recv_handed,
+    edges,
+    picked_edges,
+    owned_edges,
+    send_edge,
+    recv_edge,
+    send_picked,
+    recv_picked,
 ):
     me = lax.axis_index("seq")
     lane_blocks = state_ref.shape[1] // 128
@@ -107,6 +117,41 @@
             device_id_type=MESH,
         )
 
+    first_of_group = (me // group) * group
+    member = me % group
+    level = me // group
+    levels = n // group
+
+    def edge_to(other):
+        return pltpu.make_async_remote_copy(
+            src_ref=edge_ref,
+            dst_ref=edges.at[level],
+            send_sem=send_edge.at[other],
+            recv_sem=recv_edge.at[level],
+            device_id={"seq": other * group + member},
+            device_id_type=MESH,
+        )
+
+    def picked_to(other):
+        return pltpu.make_async_remote_copy(
+            src_ref=picked_edges.at[other],
+            dst_ref=owned_edges.at[member],
+            send_sem=send_picked.at[other],
+            recv_sem=recv_picked.at[member],
+            device_id={"seq": first_of_group + other},
+            device_id_type=MESH,
+        )
+
+    def around(count, own, action):
+        def run(step, _):
+            action(lax.rem(own + step, count))
+            return 0
+
+        lax.fori_loop(1, count, run, 0)
+
+    around(levels, level, lambda other: edge_to(other).start())
+    edges[level] = edge_ref[...]
+
     def send_first(step, _):
         peer = lax.rem(me + step, n)
         message_to(peer).start()
@@ -127,13 +172,50 @@
         lax.fori_loop(1, n, wait, 0)
 
     arrived(None, lambda peer: messages.at[peer], recv_message)
+    around(
+        levels,
+        level,
+        lambda other: pltpu.make_async_copy(
+            edges.at[other], edges.at[other], recv_edge.at[other]
+        ).wait(),
+    )
+
+    def pick_edges(step, _):
+        other = lax.rem(member + step, group)
+        for slot in range(2):
+            wanted = messages[first_of_group + other, :, pl.ds(256 + 128 * slot, 128)]
+            picked = jnp.zeros(edge_ref.shape, jnp.float32)
+            for upper in range(levels):
+                ended = end_ref[upper * group + member].astype(jnp.float32)
+                picked = jnp.where(wanted == ended, edges[upper].astype(jnp.float32), picked)
+            picked_edges[other, slot] = picked.astype(jnp.bfloat16)
+
+        @pl.when(step > 0)
+        def _():
+            picked_to(other).start()
+
+        return 0
+
+    lax.fori_loop(0, group, pick_edges, 0)
+    owned_edges[member] = picked_edges[member]
     arrived(None, lambda peer: parts.at[peer], recv_part)
 
     key_row = (me // lane_blocks) * rows
-    lanes = lax.broadcasted_iota(jnp.int32, (rows, 128), 1)
-    sublanes = lax.broadcasted_iota(jnp.int32, (rows, 128), 0)
+    tall = min(rows, 128)
+    lanes = lax.broadcasted_iota(jnp.int32, (tall, 128), 1)
+    sublanes = lax.broadcasted_iota(jnp.int32, (tall, 128), 0)
     offset = key_row % 128 + sublanes
-    key_lanes = pl.ds(pl.multiple_of((key_row // 128) * 128, 128), 128)
+
+    def decay_column(index):
+        columns = []
+        for part in range(rows // tall):
+            first = pl.multiple_of((key_row // 128 + part) * 128, 128)
+            row = messages[index, :, pl.ds(first, 128)]
+            columns.append(
+                jnp.sum(jnp.where(lanes == offset, row, 0.0), axis=1, keepdims=True)
+            )
+        return columns[0] if len(columns) == 1 else jnp.concatenate(columns, axis=0)
+
     zero = jnp.zeros((rows, 128), jnp.float32)
 
     def scan(index, carry):
@@ -145,8 +227,7 @@
         def _():
             back_to(index).start()
 
-        row = messages[index, :, key_lanes]
-        decay = jnp.sum(jnp.where(lanes == offset, row, 0.0), axis=1, keepdims=True)
+        decay = decay_column(index)
         running = decay * running + parts[index].astype(jnp.float32)
         ended = end_ref[index]
         finals = tuple(jnp.where(ended == p, running, f) for p, f in enumerate(finals))
@@ -178,6 +259,20 @@
     arrived(None, lambda peer: owned.at[(slice(None),) + block_of(peer)], recv_handed)
     owned_ref[...] = owned[...].astype(jnp.float32)
 
+    around(
+        group,
+        member,
+        lambda other: pltpu.make_async_copy(
+            owned_edges.at[other], owned_edges.at[other], recv_picked.at[other]
+        ).wait(),
+    )
+    total = owned_edges[0].astype(jnp.float32)
+    for other in range(1, group):
+        total = total + owned_edges[other].astype(jnp.float32)
+    owned_edge_ref[...] = total.astype(jnp.bfloat16)
+    around(levels, level, lambda other: edge_to(other).wait_send())
+    around(group, member, lambda other: picked_to(other).wait_send())
+
     def drain(step, _):
         peer = lax.rem(me + step, n)
         message_to(peer).wait_send()
@@ -189,24 +284,26 @@
     lax.fori_loop(1, n, drain, 0)
 
 
-def handoff(state, decay, wanted, starts_here, ends_here):
+def handoff(state, decay, edge, wanted, starts_here, ends_here):
     n = lax.axis_size("seq")
+    group = 8 if n % 8 == 0 else n // 2
     keys, values = state.shape
     rows = keys * (values // 128) // n
     message = jnp.concatenate(
-        [decay[None], jnp.broadcast_to(wanted.astype(jnp.float32)[:, None], (2, 128)).reshape(1, 256)],
+        [decay, jnp.broadcast_to(wanted.astype(jnp.float32)[:, None], (2, 128)).reshape(1, 256)],
         axis=1,
     )
     vmem = pl.BlockSpec(memory_space=pltpu.VMEM)
     smem = pl.BlockSpec(memory_space=pltpu.SMEM)
     return pl.pallas_call(
-        functools.partial(handoff_kernel, n, rows),
+        functools.partial(handoff_kernel, n, group, rows),
         out_shape=(
             jax.ShapeDtypeStruct((keys, values), jnp.bfloat16),
             jax.ShapeDtypeStruct((2, keys, values), jnp.float32),
+            jax.ShapeDtypeStruct((2,) + edge.shape, jnp.bfloat16),
         ),
-        in_specs=[smem, smem, vmem, vmem],
-        out_specs=(vmem, vmem),
+        in_specs=[smem, smem, vmem, vmem, vmem],
+        out_specs=(vmem, vmem, vmem),
         scratch_shapes=[
             pltpu.VMEM((n, rows, 128), jnp.bfloat16),
             pltpu.VMEM((n, 1, 512), jnp.float32),
@@ -215,33 +312,140 @@
             pltpu.VMEM((keys, values), jnp.bfloat16),
             pltpu.VMEM((2, keys, values), jnp.bfloat16),
         ]
-        + [pltpu.SemaphoreType.DMA((n,))] * 8,
+        + [pltpu.SemaphoreType.DMA((n,))] * 8
+        + [
+            pltpu.VMEM((n // group,) + edge.shape, jnp.bfloat16),
+            pltpu.VMEM((group, 2) + edge.shape, jnp.bfloat16),
+            pltpu.VMEM((group, 2) + edge.shape, jnp.bfloat16),
+            pltpu.SemaphoreType.DMA((n // group,)),
+            pltpu.SemaphoreType.DMA((n // group,)),
+            pltpu.SemaphoreType.DMA((group,)),
+            pltpu.SemaphoreType.DMA((group,)),
+        ],
         compiler_params=pltpu.CompilerParams(collective_id=0, has_side_effects=True),
         name="state_handoff",
-    )(starts_here, ends_here, state.astype(jnp.bfloat16), message)
-
-
-def block_pass(carry, pieces):
-    passed_along_state, offset = carry
-    q_blk, k_blk, value_block, decay_blk = pieces
-    block_rows = q_blk.shape[0]
-    k_wide = k_blk.astype(jnp.float32)
-    cumulative = jnp.cumsum(decay_blk, axis=0)
-    query_decayed = (q_blk * jnp.exp(cumulative)).astype(jnp.bfloat16)
-    pair_decay = jnp.exp(jnp.minimum(cumulative[:, None] - cumulative[None, :], 0.0))
-    causal_mask = jnp.arange(block_rows)[:, None] >= jnp.arange(block_rows)[None, :]
-    scores = jnp.einsum("ihk,jhk,ijhk->hij", q_blk, k_wide, pair_decay, precision=EXACT_MATMUL)
-    scores = jnp.where(causal_mask[None], scores, 0.0).astype(jnp.bfloat16)
-    intra_term = jnp.einsum("hij,jhv->ihv", scores, value_block, preferred_element_type=jnp.float32)
-    closing_decay = cumulative[-1]
-    weight_applied = (k_wide * jnp.exp(closing_decay[None] - cumulative)).astype(jnp.bfloat16)
-    updated = jnp.exp(closing_decay)[:, :, None] * passed_along_state + jnp.einsum(
-        "qbr,qbp->brp", weight_applied, value_block, preferred_element_type=jnp.float32
-    )
-    return (
-        (updated, offset + closing_decay),
-        (intra_term, passed_along_state, offset, query_decayed),
-    )
+    )(starts_here, ends_here, state, message, edge)
+
+
+def local_kernel(
+    live_ref,
+    projected_ref,
+    low_rank_ref,
+    gate_up_ref,
+    gate_bias_ref,
+    conv_ref,
+    out_ref,
+    query_ref,
+    state_ref,
+    decay_ref,
+    state,
+    offset,
+):
+    rows = out_ref.shape[0]
+    keys, values = state.shape
+    halo = projected_ref.shape[0] - rows
+    taps = conv_ref.shape[0]
+    state[...] = jnp.zeros_like(state)
+    offset[...] = jnp.zeros_like(offset)
+    row_of = lax.broadcasted_iota(jnp.int32, (STRETCH, 1), 0)
+    at_row = lax.broadcasted_iota(jnp.int32, (STRETCH, STRETCH), 0)
+    at_col = lax.broadcasted_iota(jnp.int32, (STRETCH, STRETCH), 1)
+    lower = (at_row >= at_col).astype(jnp.float32)
+    ones = jnp.ones((STRETCH, 128), jnp.float32)
+
+    def contract(a, b, dims, precision=None):
+        return lax.dot_general(
+            a, b, (dims, ((), ())), precision=precision, preferred_element_type=jnp.float32
+        )
+
+    def one_block(block, _):
+        base = pl.multiple_of(block * STRETCH, STRETCH)
+        here = pl.ds(base, STRETCH)
+        window = projected_ref[pl.ds(base, STRETCH + halo), :].astype(jnp.float32)
+        total = jnp.zeros((STRETCH, window.shape[1]), jnp.float32)
+        for tap in range(taps):
+            first = halo - taps + 1 + tap
+            total = total + conv_ref[tap : tap + 1, :] * window[first : first + STRETCH]
+        activated = (total * jax.nn.sigmoid(total)).astype(jnp.bfloat16)
+        valid = base + row_of < live_ref[0]
+        query = activated[:, :keys].astype(jnp.float32) * keys ** (-0.5)
+        key = jnp.where(valid, activated[:, keys : 2 * keys].astype(jnp.float32), 0.0)
+        value = activated[:, 2 * keys :]
+        logits = contract(
+            low_rank_ref[here, :], gate_up_ref[...], ((1,), (0,)), EXACT_MATMUL
+        ) + gate_bias_ref[...]
+        log_decay = (jnp.minimum(logits, 0.0) - jnp.log1p(jnp.exp(-jnp.abs(logits)))) / 16.0
+        log_decay = jnp.where(valid, log_decay, 0.0)
+        running = contract(lower, log_decay, ((1,), (0,)), EXACT_MATMUL)
+        closing = running[STRETCH - 1 : STRETCH]
+        closing_column = contract(log_decay, ones, ((0,), (0,)), EXACT_MATMUL)
+
+        scores = jnp.zeros((STRETCH, STRETCH), jnp.float32)
+        half = STRETCH // 2
+        while half >= 8:
+            pair = 2 * half
+            pieces = []
+            for first in range(0, STRETCH, pair):
+                middle = running[first + half - 1 : first + half]
+                pieces.append(jnp.broadcast_to(middle, (pair, keys)))
+            middle = pieces[0] if len(pieces) == 1 else jnp.concatenate(pieces, axis=0)
+            factor = jnp.exp(-jnp.abs(running - middle))
+            second = row_of % pair >= half
+            left = jnp.where(second, query * factor, 0.0).astype(jnp.bfloat16)
+            right = jnp.where(second, 0.0, key * factor).astype(jnp.bfloat16)
+            part = contract(left, right, ((1,), (1,)))
+            scores = scores + jnp.where(at_row // pair == at_col // pair, part, 0.0)
+            half //= 2
+        for shift in range(8):
+            if shift:
+                moved_key = pltpu.roll(key, shift, 0)
+                moved_sum = pltpu.roll(running, shift, 0)
+                product = query * moved_key * jnp.exp(jnp.minimum(running - moved_sum, 0.0))
+            else:
+                product = query * key
+            summed = jnp.sum(product, axis=1, keepdims=True)
+            chosen = (at_col == at_row - shift) & (at_row % 8 >= shift)
+            scores = scores + jnp.where(chosen, summed, 0.0)
+
+        decayed = (query * jnp.exp(running)).astype(jnp.bfloat16)
+        weighted = (key * jnp.exp(closing - running)).astype(jnp.bfloat16)
+        query_ref[here, :] = (query * jnp.exp(running + offset[...])).astype(jnp.bfloat16)
+        before = state[...]
+        out_ref[here, :] = contract(
+            scores.astype(jnp.bfloat16), value, ((1,), (0,))
+        ) + contract(decayed, before.astype(jnp.bfloat16), ((1,), (0,)))
+        factor = jnp.exp(closing_column)
+        factor = jnp.concatenate([factor] * (values // 128), axis=1)
+        state[...] = factor * before + contract(weighted, value, ((0,), (0,)))
+        offset[...] = offset[...] + closing
+        return 0
+
+    lax.fori_loop(0, rows // STRETCH, one_block, 0)
+    state_ref[...] = state[...].astype(jnp.bfloat16)
+    decay_ref[...] = jnp.exp(offset[...])
+
+
+def local_blocks(live_rows, projected, low_rank, gate_up, gate_bias, conv_weight, values):
+    rows = low_rank.shape[0]
+    keys = gate_up.shape[1]
+    vmem = pl.BlockSpec(memory_space=pltpu.VMEM)
+    smem = pl.BlockSpec(memory_space=pltpu.SMEM)
+    return pl.pallas_call(
+        local_kernel,
+        out_shape=(
+            jax.ShapeDtypeStruct((rows, values), jnp.float32),
+            jax.ShapeDtypeStruct((rows, keys), jnp.bfloat16),
+            jax.ShapeDtypeStruct((keys, values), jnp.bfloat16),
+            jax.ShapeDtypeStruct((1, keys), jnp.float32),
+        ),
+        in_specs=[smem] + [vmem] * 5,
+        out_specs=(vmem,) * 4,
+        scratch_shapes=[
+            pltpu.VMEM((keys, values), jnp.float32),
+            pltpu.VMEM((1, keys), jnp.float32),
+        ],
+        name="local_blocks",
+    )(live_rows.reshape(1), projected, low_rank, gate_up, gate_bias, conv_weight)
 
 
 def body(
@@ -294,69 +498,36 @@
     projected = qkv_sum.astype(jnp.bfloat16).reshape(row_count, local_heads, width_qkv)
     gate_rounded = lax.optimization_barrier(gate_sum.astype(jnp.bfloat16))
     gate_values = gate_rounded.astype(jnp.float32).reshape(row_count, local_heads, value_width)
-    logits = jnp.dot(
-        low_rank, gate_up.reshape(gate_up.shape[0], local_heads * key_width), precision=EXACT_MATMUL
-    )
-    logits = logits.reshape(row_count, local_heads, key_width) + gate_bias[None]
-    log_decay = jnp.where(valid[:, None, None], jax.nn.log_sigmoid(logits) / 16.0, 0.0)
     tail_rows = projected[row_count - taps + 1 :]
     previous = from_behind(tail_rows, "seq", 1)
     previous = jnp.where(is_start, jnp.zeros_like(previous), previous)
-    extended = jnp.concatenate([previous, projected], axis=0)
-    conv_sum = jnp.zeros((row_count, local_heads, width_qkv), jnp.float32)
-    for offset in range(taps):
-        conv_sum = conv_sum + conv_weight[offset][None] * extended[
-            offset : offset + row_count
-        ].astype(jnp.float32)
-    activated = jax.nn.silu(conv_sum).astype(jnp.bfloat16)
-    query_rows = activated[:, :, :key_width].astype(jnp.float32) * key_width ** (-0.5)
-    key_rows = jnp.where(
-        valid[:, None, None],
-        activated[:, :, key_width : 2 * key_width],
-        jnp.zeros((), jnp.bfloat16),
-    )
-    value_rows = activated[:, :, 2 * key_width :]
-
-    def into_blocks(array):
-        return array.reshape(row_count // STRETCH, STRETCH, local_heads, array.shape[-1])
-
-    start_carry = (
-        jnp.zeros((local_heads, key_width, value_width), jnp.float32),
-        jnp.zeros((local_heads, key_width), jnp.float32),
-    )
-    (local_state, decay_sum), (local_out, block_starts, block_offsets, query_decayed) = lax.scan(
-        block_pass,
-        start_carry,
-        (
-            into_blocks(query_rows),
-            into_blocks(key_rows),
-            into_blocks(value_rows),
-            into_blocks(log_decay),
-        ),
-    )
+    halo = 16
+    front = jnp.zeros((halo - taps + 1, width_qkv), jnp.bfloat16)
+    extended = jnp.concatenate([front, previous[:, 0], projected[:, 0]], axis=0)
+    local_out, query_decayed, local_state, decay = local_blocks(
+        live_rows, extended, low_rank, gate_up[:, 0], gate_bias, conv_weight[:, 0], value_width
+    )
+    edge_rows = lax.dynamic_slice_in_dim(extended, live_rows + halo - taps + 1, taps - 1, 0)
+    edge = jnp.pad(edge_rows.reshape(-1, 128), ((0, 8), (0, 0)))
     devices = jnp.arange(lax.axis_size("seq"), dtype=jnp.int32)
     starts_here = jnp.any(devices[:, None] == starts[None, :], axis=1).astype(jnp.int32)
     ends_here = jnp.sum(
         jnp.where(
             devices[:, None] == span_ends[None, :] - 1,
-            jnp.arange(prompts, dtype=jnp.int32)[None, :] + 1,
+            jnp.arange(prompts, dtype=jnp.int32)[None, :] + 2,
             0,
         ),
         axis=1,
-    ) - 1
-    incoming, owner_state = handoff(
-        local_state[0], jnp.exp(decay_sum)[0], request_prompt, starts_here, ends_here
-    )
-    incoming = incoming.astype(jnp.float32)[None]
+    ) - 2
+    incoming, owner_state, owned_edge = handoff(
+        local_state, decay, edge, request_prompt, starts_here, ends_here
+    )
     owner_state = owner_state[:, None]
-    full_starts = block_starts + jnp.exp(block_offsets)[:, :, :, None] * incoming[None]
-    cross_block_term = jnp.einsum(
-        "bchk,bhkv->bchv",
-        query_decayed,
-        full_starts.astype(jnp.bfloat16),
-        preferred_element_type=jnp.float32,
-    )
-    attended = (cross_block_term + local_out).reshape(row_count, local_heads, value_width)
+    owner_edge = owned_edge[:, : edge.shape[0] - 8].reshape(
+        slot_count, taps - 1, local_heads, width_qkv
+    )
+    attended = local_out + jnp.dot(query_decayed, incoming, preferred_element_type=jnp.float32)
+    attended = attended.reshape(row_count, local_heads, value_width)
     mean_square = jnp.mean(attended * attended, axis=2, keepdims=True)
     gated = (
         attended
@@ -374,12 +545,6 @@
     ).astype(jnp.float32)
     own_rows = lax.axis_index("tensor") * share + jnp.arange(share, dtype=jnp.int32)
     mixed = jnp.where((own_rows < live_rows)[:, None], summed, 0.0).astype(jnp.bfloat16)
-    edge_rows = lax.dynamic_slice_in_dim(extended, live_rows, taps - 1, 0)
-    ending = (is_last & picked)[:, None, None, None]
-    edges = lax.psum(jnp.where(ending, edge_rows[None], jnp.zeros((), jnp.bfloat16)), "seq")
-    owner_edge = jnp.zeros((slot_count,) + edge_rows.shape, jnp.bfloat16)
-    for p in range(prompts):
-        owner_edge = jnp.where((request_prompt == p)[:, None, None, None], edges[p][None], owner_edge)
     return (mixed, owner_state, owner_edge)
 
 

time: 443 us -> 172 us (0.39)
  blocking collectives: 255 us -> 9.29 us
  other arithmetic: 49.9 us -> 10.1 us
  waiting for transfers between devices: 20.8 us -> 47.6 us
  Pallas kernels: 50.4 us -> 65.1 us
  matrix products: 24.6 us -> 13.5 us
  local copies, waits for them, and re-layouts: 16.7 us -> 6.02 us
    psum x1 -> x0, blocking collectives: 245 us -> none  [body(): lax.psum(jnp.where(ending, edge_rows[None], jnp.zeros((), jnp.bfloat16)),...]
    reduce_scatter x1, waiting for transfers between devices: 0.01 us -> 28.5 us  [body(): lax.psum_scatter(jnp.dot(gated, w_out, preferred_element_type=jnp.float32...]
    while x8 -> x0, other arithmetic: 19.3 us -> none
    pallas_call x1 -> x2, Pallas kernels: 50.4 us -> 65.1 us  [the longest x1 52.3 us: handoff(): pl.pallas_call(functools.partial(handoff_kernel, n, group, rows), out_sha...]
    dot_general x18 -> x1, matrix products: 13.8 us -> 1.77 us  [body(): jnp.dot(query_decayed, incoming, preferred_element_type=jnp.float32)]
    dynamic_slice x16 -> x1, local copies, waits for them, and re-layouts: 7.2 us -> 0.02 us  [body(): lax.dynamic_slice_in_dim(extended, live_rows + halo - taps + 1, taps - 1, 0)]
    dynamic_update_slice x16 -> x0, other arithmetic: 6.83 us -> none  [body(): lax.scan(block_pass, start_carry, (into_blocks(query_rows), into_blocks(k...]
    convert_element_type x20 -> x0, other arithmetic: 6.56 us -> none  [the longest x8 1.5 us: block_pass(): query_decayed = (q_blk * jnp.exp(cumulative)).astype(jnp.bfloat16)]
  transfers between devices with their start and end apart: 3 -> 3, of which waited for: 1 -> 2; matrix products, arithmetic and copies ran while one was open for 3% -> 8% of each run, Pallas kernels for 0% -> 0%
where the time goes in v2:
time: 172 us
  Pallas kernels  65.1 us (38%)
  waiting for transfers between devices  47.6 us (28%)
  between operations  16.1 us (9%)
  matrix products  13.5 us (8%)
  other arithmetic  10.1 us (6%)
  blocking collectives  9.29 us (5%)
  local copies, waits for them, and re-layouts  6.02 us (4%)
  starting transfers between devices  4.05 us (2%)
    pallas_call x1, Pallas kernels, handoff(): pl.pallas_call(functools.partial(handoff_kernel, n, group, rows), out_sha...  52.3 us
    reduce_scatter x1, waiting for transfers between devices, body(): lax.psum_scatter(jnp.dot(gated, w_out, preferred_element_type=jnp.float32...  28.5 us
    all_gather x1, waiting for transfers between devices, body(): lax.all_gather(tokens, 'tensor', axis=1, tiled=True).astype(jnp.float32)  18.4 us
    pallas_call x1, Pallas kernels, local_blocks(): pl.pallas_call(local_kernel, out_shape=(jax.ShapeDtypeStruct((rows, value...  12.7 us
    psum x1, blocking collectives, body(): squares = lax.psum(jnp.sum(value_entries * value_entries, axis=1), 'tensor')  9.29 us
    dot_general x1, matrix products, body(): qkv_sum = jnp.dot(normed, flat_qkv, preferred_element_type=jnp.float32)  5.35 us
    unnamed x24, local copies, waits for them, and re-layouts  5.19 us
    ppermute x1, starting transfers between devices, from_behind(): return lax.ppermute(array, axis, pairs)  3.97 us
  transfers between devices with their start and end apart: 3, of which 2 were waited for; matrix products, arithmetic and copies ran while one was open for 8% of the time, Pallas kernels for 0%

profile of v2, /device:TPU:1, one launch (start us, length us, event | category | flops | bytes accessed | tf_op | source)
XLA Modules:
  0.0 171.8 jit_solution(16909715070453720310)
XLA Ops:
  7.2 0.0 copy-start
  7.2 0.0 all-gather.2.cloned.1.call-start
  7.2 0.7 all-gather.2.cloned.1.call-update
  7.9 0.0 reduce-scatter.2.cloned.1.call-start
  8.0 0.7 convert_element_type.48
  8.6 0.8 reduce-window.7
  9.4 0.6 fusion.15
  10.1 2.0 %bitcast_add_fusion = (s32[3]{0:T(128)S(1)}, s32[]{:T(128)}, s32[]{:T(128)}, s32[3]{0:T(128)S(1)}, s32[]{:T(128)}) fusion(s32[3,1]{0,1:T(1,128)S(1)} %reduce-window.7, s32[]{:T(128)} %fusion.15, s32[3]{0:T(128)} %param.23, s32[3]{0:T(128)} %param.24), kind=kLoop, calls=%fused_computation.35 | loop fusion | flops 24 | bytes 76 | tf_op jit(solution)/shard_map/sub | solution.py:481
  14.0 0.1 fusion.14
  14.1 0.5 convert_element_type.47.start_ref
  14.6 1.3 copy.35
  15.9 1.3 copy.34
  17.2 1.2 multiply_reduce_fusion.1
  18.4 9.3 %psum.7 = f32[512]{0:T(512)S(1)} all-reduce(f32[512]{0:T(512)S(1)} %multiply_reduce_fusion.1), channel_id=1, replica_groups=mesh['seq'=64,'tensor'=4] {'tensor'}, use_global_device_ids=true, to_apply=%region_6.7 | all-reduce | flops 512 | bytes 4096 | tf_op jit(solution)/shard_map/psum | solution.py:487
  27.7 0.1 select_reduce_fusion
  27.8 0.5 broadcast_add_fusion.end_ref
  28.4 0.0 copy-start.7
  28.4 18.4 %all-gather.2.cloned.1.call-done = bf16[512,2048]{1,0:T(8,128)(2,1)} async-done(((bf16[512,512]{1,0:T(8,128)(2,1)}), bf16[512,2048]{1,0:T(8,128)(2,1)}) %all-gather.2.cloned.1.call-update) | async-done | bytes 2097168 | tf_op jit(solution)/shard_map/all_gather | solution.py:491
  46.8 0.0 copy-start.4
  46.8 0.0 copy-start.5
  46.8 5.4 %fusion.2 = bf16[512,1024]{1,0:T(8,128)(2,1)S(1)} fusion(bf16[2048,1,1024]{2,0,1:T(8,128)(2,1)} %param.15, bf16[512,2048]{1,0:T(8,128)(2,1)} %all-gather.2.cloned.1.call-done, f32[2048]{0:T(1024)} %param.14, f32[512]{0:T(512)S(1)} %add_rsqrt_fusion.1), kind=kOutput, calls=%fused_computation.4 | convolution fusion | flops 2152202240 | bytes 7350272 | tf_op jit(solution)/shard_map/dot_general | solution.py:495
  52.2 0.0 copy-start.6
  52.2 4.0 %collective-permute-start = (bf16[3,1,1024]{2,0,1:T(4,128)(2,1)S(1)}, bf16[3,1,1024]{2,0,1:T(4,128)(2,1)S(1)}, u32[]{:S(2)}, u32[]{:S(2)}) collective-permute-start(bf16[3,1,1024]{2,0,1:T(4,128)(2,1)S(1)} %slice_bitcast_fusion), channel_id=1, source_target_pairs={{0,4},{4,8},{8,12},{12,16},{16,20},{20,24},{24,28},{28,32},{32,36}... | collective-permute-start | bytes 18440 | tf_op jit(solution)/shard_map/ppermute | solution.py:22
  56.2 0.0 copy-done.7
  56.2 0.0 copy-done.4
  56.2 0.0 copy-done.5
  56.2 2.1 %convolution_convert_fusion.1 = bf16[512,512]{1,0:T(8,128)(2,1)} fusion(bf16[2048,512]{1,0:T(8,128)(2,1)S(1)} %copy-done.4, bf16[512,2048]{1,0:T(8,128)(2,1)S(1)} %copy-done.5, f32[2048]{0:T(1024)S(1)} %copy-done.7, f32[512]{0:T(512)S(1)} %add_rsqrt_fusion.1), kind=kOutput, calls=%fused_computation.8 | convolution fusion | flops 1078198272 | bytes 4728832 | tf_op jit(solution)/shard_map/dot_general | solution.py:496
  58.3 0.0 copy-done.6
  58.3 1.5 fusion.17.low_rank_ref
  59.8 0.0 collective-permute-done
  59.8 0.2 pad_maximum_fusion.projected_ref
  60.0 0.0 copy-start.1
  60.1 0.7 pad.4.edge_ref
  60.8 0.3 copy-done.1
  61.0 0.0 copy-start.8
  61.0 12.7 %local_blocks.1 = (f32[512,512]{1,0:T(8,128)}, bf16[512,256]{1,0:T(8,128)(2,1)}, bf16[256,512]{1,0:T(8,128)(2,1)}, f32[1,256]{1,0:T(1,128)}) custom-call(s32[1]{0:T(128)} %bitcast.2.live_ref, bf16[528,1024]{1,0:T(8,128)(2,1)} %copy-done.1, f32[512,16]{1,0:T(8,128)} %fusion.17.low_rank_ref, f32[16,256]{1,0:T(8,128)} %bitcast.34, f32[1,256]{1,0:T(1,128)} %gate_bias_ref.1, ...), custom_call_target="tpu_custom_call" | custom-call | tf_op jit(solution)/shard_map/local_blocks/pallas_call | solution.py:433
  73.8 0.0 copy-start.9
  73.8 0.1 broadcast_in_dim.61
  73.9 1.3 pad_maximum_fusion.1.message_ref
  75.1 52.3 %state_handoff.1 = (bf16[256,512]{1,0:T(8,128)(2,1)}, f32[2,256,512]{2,1,0:T(8,128)}, bf16[2,32,128]{2,1,0:T(8,128)(2,1)}) custom-call(s32[64]{0:T(128)} %convert_element_type.47.start_ref, s32[64]{0:T(128)} %broadcast_add_fusion.end_ref, bf16[256,512]{1,0:T(8,128)(2,1)} %get-tuple-element.12.state_ref, f32[1,512]{1,0:T(1,128)} %pad_maximum_fusion.1.message_ref, ...), custom_call_target="tpu_custom_call" | custom-call | tf_op jit(solution)/shard_map/state_handoff/pallas_call | solution.py:298
  127.5 1.8 %multiply_reduce_fusion = (f32[512]{0:T(512)S(1)}, f32[512,512]{1,0:T(8,128)S(1)}) fusion(f32[512,512]{1,0:T(8,128)} %get-tuple-element.10, bf16[512,256]{1,0:T(8,128)(2,1)} %get-tuple-element.11, bf16[256,512]{1,0:T(8,128)(2,1)} %get-tuple-element.14), kind=kOutput, calls=%fused_computation.15 | convolution fusion | flops 135003648 | bytes 2623488 | tf_op jit(solution)/shard_map/dot_general | solution.py:529
  129.3 0.0 copy-done
  129.3 0.0 copy-done.8
  129.3 0.0 copy-done.9
  129.3 2.8 %convolution_convert_fusion = bf16[512,2048]{1,0:T(8,128)(2,1)} fusion(bf16[512,2048]{1,0:T(8,128)(2,1)S(1)} %copy-done, bf16[512,512]{1,0:T(8,128)(2,1)S(1)} %copy-done.9, f32[512,512]{1,0:T(8,128)S(1)} %get-tuple-element.33, f32[512]{0:T(512)S(1)} %copy-done.8, f32[512]{0:T(512)S(1)} %add_rsqrt_fusion), kind=kOutput, calls=%fused_computation.3 | convolution fusion | flops 1077149696 | bytes 5771264 | tf_op jit(solution)/shard_map/dot_general | solution.py:541
  132.1 0.0 copy-start.3
  132.1 0.0 copy-start.2
  132.1 0.0 reduce-scatter.2.cloned.1.call-update
  132.2 0.7 copy-done.3
  132.9 0.6 copy.27
  133.5 28.5 %reduce-scatter.2.cloned.1.call-done = bf16[128,2048]{1,0:T(8,128)(2,1)} async-done(((bf16[512,2048]{1,0:T(8,128)(2,1)}), bf16[128,2048]{1,0:T(8,128)(2,1)}) %reduce-scatter.2.cloned.1.call-update) | async-done | bytes 524304 | tf_op jit(solution)/shard_map/reduce_scatter | solution.py:540
  162.0 2.0 %select_convert_fusion = bf16[128,2048]{1,0:T(8,128)(2,1)} fusion(bf16[128,2048]{1,0:T(8,128)(2,1)} %reduce-scatter.2.cloned.1.call-done, pred[128]{0:T(512)(128)(4,1)S(1)} %add_compare_fusion), kind=kLoop, calls=%fused_computation.14 | loop fusion | flops 786432 | bytes 1048704 | tf_op jit(solution)/shard_map/convert_element_type | solution.py:547
  163.9 0.0 copy-done.2
  163.9 1.0 copy.37
  (12 shorter events, 0.1 us)
Async XLA Ops:
  7.2 122.1 %copy-start = (bf16[512,2048]{1,0:T(8,128)(2,1)S(1)}, bf16[512,2048]{1,0:T(8,128)(2,1)}, u32[]{:S(2)}) copy-start(bf16[512,2048]{1,0:T(8,128)(2,1)} %param.22) | copy-start | bytes 6291460
  7.2 39.6 %all-gather.2.cloned.1.call-start = ((), (), s32[]{:S(2)}) async-start(), calls=%async_computation.1 | async-start | bytes 2621440 | tf_op jit(solution)/shard_map/all_gather | solution.py:491
  7.9 154.0 %reduce-scatter.2.cloned.1.call-start = ((), (), s32[]{:S(2)}) async-start(), calls=%async_computation.2 | async-start | bytes 2621440 | tf_op jit(solution)/shard_map/reduce_scatter | solution.py:540
  28.4 27.8 %copy-start.7 = (f32[2048]{0:T(1024)S(1)}, f32[2048]{0:T(1024)}, u32[]{:S(2)}) copy-start(f32[2048]{0:T(1024)} %param.14) | copy-start | bytes 24580
  46.8 9.4 %copy-start.4 = (bf16[2048,512]{1,0:T(8,128)(2,1)S(1)}, bf16[2048,512]{1,0:T(8,128)(2,1)}, u32[]{:S(2)}) copy-start(bf16[2048,512]{1,0:T(8,128)(2,1)} %param.16) | copy-start | bytes 6291460
  46.8 9.4 %copy-start.5 = (bf16[512,2048]{1,0:T(8,128)(2,1)S(1)}, bf16[512,2048]{1,0:T(8,128)(2,1)}, u32[]{:S(2)}) copy-start(bf16[512,2048]{1,0:T(8,128)(2,1)} %all-gather.2.cloned.1.call-done) | copy-start | bytes 6291460
  52.2 6.1 %copy-start.6 = (bf16[2048,16]{0,1:T(8,128)(2,1)S(1)}, bf16[2048,16]{0,1:T(8,128)(2,1)}, u32[]{:S(2)}) copy-start(bf16[2048,16]{0,1:T(8,128)(2,1)} %param.17) | copy-start | bytes 196612
  52.2 7.6 %collective-permute-start = (bf16[3,1,1024]{2,0,1:T(4,128)(2,1)S(1)}, bf16[3,1,1024]{2,0,1:T(4,128)(2,1)S(1)}, u32[]{:S(2)}, u32[]{:S(2)}) collective-permute-start(bf16[3,1,1024]{2,0,1:T(4,128)(2,1)S(1)} %slice_bitcast_fusion), channel_id=1, source_target_pairs={{0,4},{4,8},{8,12},{12,16},{16,20},{20,24},{24,28},{28,32},{32,36}... | collective-permute-start | bytes 18440 | tf_op jit(solution)/shard_map/ppermute | solution.py:22
  60.0 1.0 copy-start.1
  61.0 68.2 %copy-start.8 = (f32[512]{0:T(512)S(1)}, f32[512]{0:T(512)}, u32[]{:S(2)}) copy-start(f32[512]{0:T(512)} %param.21) | copy-start | bytes 6148
  73.8 55.5 %copy-start.9 = (bf16[512,512]{1,0:T(8,128)(2,1)S(1)}, bf16[512,512]{1,0:T(8,128)(2,1)}, u32[]{:S(2)}) copy-start(bf16[512,512]{1,0:T(8,128)(2,1)} %convolution_convert_fusion.1) | copy-start | bytes 1572868
  132.1 0.7 copy-start.3
  132.1 31.8 %copy-start.2 = (f32[2,256,512]{2,1,0:T(8,128)S(1)}, f32[2,256,512]{2,1,0:T(8,128)}, u32[]{:S(2)}) copy-start(f32[2,256,512]{2,1,0:T(8,128)} %get-tuple-element.15) | copy-start | bytes 3145732
Sparse Core Ops, SparseCore 0:
  9.8 36.9 all-gather.1
  132.3 29.6 reduce-scatter.1

commit v3 on v2

--- a/solution.py
+++ b/solution.py
@@ -16,10 +16,195 @@
 MESH = pl.DeviceIdType.MESH
 
 
-def from_behind(array, axis, by):
-    peers = lax.axis_size(axis)
-    pairs = [(i, i + by) for i in range(peers) if 0 <= i + by < peers]
-    return lax.ppermute(array, axis, pairs)
+HALO = 16
+CHUNKS = ((16, 96, 176), (176, 272, 352), (352, 448, 528))
+
+
+def neighbours():
+    n = lax.axis_size("tensor")
+    x = lax.axis_index("tensor")
+    return x, lax.rem(x + 1, n), lax.rem(x + n - 1, n), lax.rem(x + 2, n)
+
+
+def project_kernel(
+    start_ref,
+    tokens_ref,
+    gain_ref,
+    qkv_hbm,
+    gate_hbm,
+    down_ref,
+    projected_ref,
+    gate_ref,
+    low_rank_ref,
+    gathered,
+    normed,
+    qkv,
+    gate,
+    load_sem,
+    send_right,
+    send_left,
+    from_left,
+    from_right,
+    pass_right,
+    pass_left,
+    far_left,
+    far_right,
+    send_halo,
+    recv_halo,
+):
+    n = lax.axis_size("seq")
+    peers = lax.axis_size("tensor")
+    me = lax.axis_index("seq")
+    x, right, left, far = neighbours()
+    after, before = lax.rem(me + 1, n), lax.rem(me + n - 1, n)
+    width = tokens_ref.shape[1]
+    loads = [
+        pltpu.make_async_copy(qkv_hbm, qkv, load_sem.at[0]),
+        pltpu.make_async_copy(gate_hbm, gate, load_sem.at[1]),
+    ]
+    for load in loads:
+        load.start()
+
+    barrier = pltpu.get_barrier_semaphore()
+    for peer in (right, left):
+        pl.semaphore_signal(barrier, inc=1, device_id={"tensor": peer}, device_id_type=MESH)
+    for peer in range(peers):
+        pl.semaphore_signal(
+            barrier, inc=1, device_id={"seq": before, "tensor": peer}, device_id_type=MESH
+        )
+    pl.semaphore_wait(barrier, 2 + peers)
+
+    def own(chunk, to, send, recv):
+        first, _, last = CHUNKS[chunk]
+        return pltpu.make_async_remote_copy(
+            src_ref=tokens_ref.at[pl.ds(first - HALO, last - first)],
+            dst_ref=gathered.at[x, pl.ds(first, last - first)],
+            send_sem=send.at[chunk],
+            recv_sem=recv.at[chunk],
+            device_id={"tensor": to},
+            device_id_type=MESH,
+        )
+
+    def passed(chunk, owner, to, upper, send, recv):
+        first, middle, last = CHUNKS[chunk]
+        first, last = (middle, last) if upper else (first, middle)
+        ref = gathered.at[owner, pl.ds(first, last - first)]
+        return pltpu.make_async_remote_copy(
+            src_ref=ref,
+            dst_ref=ref,
+            send_sem=send.at[chunk],
+            recv_sem=recv.at[chunk],
+            device_id={"tensor": to},
+            device_id_type=MESH,
+        )
+
+    def landed(owner, first, last, sem):
+        ref = gathered.at[owner, pl.ds(first, last - first)]
+        pltpu.make_async_copy(ref, ref, sem).wait()
+
+    halos = []
+    for peer in range(peers):
+        halos.append(
+            pltpu.make_async_remote_copy(
+                src_ref=tokens_ref.at[pl.ds(tokens_ref.shape[0] - HALO, HALO)],
+                dst_ref=gathered.at[x, pl.ds(0, HALO)],
+                send_sem=send_halo.at[peer],
+                recv_sem=recv_halo.at[x],
+                device_id={"seq": after, "tensor": peer},
+                device_id_type=MESH,
+            )
+        )
+    count = len(CHUNKS)
+    rights = [own(c, right, send_right, from_left) for c in range(count)]
+    lefts = [own(c, left, send_left, from_right) for c in range(count)]
+    onward_right = [passed(c, left, right, False, pass_right, far_left) for c in range(count)]
+    onward_left = [passed(c, right, left, True, pass_left, far_right) for c in range(count)]
+    for copy in (rights[0], lefts[0], *halos, rights[1], lefts[1]):
+        copy.start()
+    gathered[x, pl.ds(HALO, tokens_ref.shape[0])] = tokens_ref[...]
+
+    def compute(chunk):
+        first = 0 if chunk == 0 else CHUNKS[chunk][0]
+        last = CHUNKS[chunk][2]
+        here = pl.ds(first, last - first)
+        squares = jnp.zeros((last - first, 1), jnp.float32)
+        for owner in range(peers):
+            piece = gathered[owner, here].astype(jnp.float32)
+            squares = squares + jnp.sum(piece * piece, axis=1, keepdims=True)
+        inverse = lax.rsqrt(squares / (width * peers) + EPS_IN)
+        for owner in range(peers):
+            lanes = pl.ds(owner * width, width)
+            piece = gathered[owner, here].astype(jnp.float32)
+            normed[:, lanes] = (piece * inverse * gain_ref[:, lanes]).astype(jnp.bfloat16)
+        rows = normed[...]
+        made = jnp.dot(rows, qkv[...], preferred_element_type=jnp.float32)
+        if chunk == 0:
+            row_of = lax.broadcasted_iota(jnp.int32, (last - first, 1), 0)
+            made = jnp.where((row_of < HALO) & (start_ref[0] == 1), 0.0, made)
+        projected_ref[here, :] = made.astype(jnp.bfloat16)
+        gate_ref[here, :] = jnp.dot(
+            rows, gate[...], preferred_element_type=jnp.float32
+        ).astype(jnp.bfloat16)
+        low_rank_ref[here, :] = jnp.dot(rows, down_ref[...], preferred_element_type=jnp.float32)
+
+    def arrive_and_compute(chunk):
+        first, middle, last = CHUNKS[chunk]
+        landed(far, first, middle, far_left.at[chunk])
+        landed(far, middle, last, far_right.at[chunk])
+        if chunk == 0:
+            for load in loads:
+                load.wait()
+            for peer in range(peers):
+                landed(peer, 0, HALO, recv_halo.at[peer])
+        compute(chunk)
+
+    for chunk in range(count):
+        first, middle, last = CHUNKS[chunk]
+        landed(left, first, last, from_left.at[chunk])
+        onward_right[chunk].start()
+        landed(right, first, last, from_right.at[chunk])
+        onward_left[chunk].start()
+        if chunk + 2 < count:
+            rights[chunk + 2].start()
+            lefts[chunk + 2].start()
+        if chunk:
+            arrive_and_compute(chunk - 1)
+    arrive_and_compute(count - 1)
+    for copy in (*rights, *lefts, *onward_right, *onward_left, *halos):
+        copy.wait_send()
+
+
+def project(is_start, tokens, norm_gain, w_qkv, w_gate_out, gate_down):
+    rows, width = tokens.shape
+    vmem = pl.BlockSpec(memory_space=pltpu.VMEM)
+    smem = pl.BlockSpec(memory_space=pltpu.SMEM)
+    anywhere = pl.BlockSpec(memory_space=pl.ANY)
+    peers = lax.axis_size("tensor")
+    tall = rows + HALO
+    count = len(CHUNKS)
+    return pl.pallas_call(
+        project_kernel,
+        out_shape=(
+            jax.ShapeDtypeStruct((tall, w_qkv.shape[1]), jnp.bfloat16),
+            jax.ShapeDtypeStruct((tall, w_gate_out.shape[1]), jnp.bfloat16),
+            jax.ShapeDtypeStruct((tall, gate_down.shape[1]), jnp.float32),
+        ),
+        in_specs=[smem, vmem, vmem, anywhere, anywhere, vmem],
+        out_specs=(vmem,) * 3,
+        scratch_shapes=[
+            pltpu.VMEM((peers, tall, width), jnp.bfloat16),
+            pltpu.VMEM((tall // count, width * peers), jnp.bfloat16),
+            pltpu.VMEM(w_qkv.shape, jnp.bfloat16),
+            pltpu.VMEM(w_gate_out.shape, jnp.bfloat16),
+            pltpu.SemaphoreType.DMA((2,)),
+        ]
+        + [pltpu.SemaphoreType.DMA((count,))] * 8
+        + [pltpu.SemaphoreType.DMA((peers,))] * 2,
+        compiler_params=pltpu.CompilerParams(
+            collective_id=1, has_side_effects=True, vmem_limit_bytes=48 * 1024 * 1024
+        ),
+        name="gather_project",
+    )(is_start.reshape(1), tokens, norm_gain.reshape(1, -1), w_qkv, w_gate_out, gate_down)
 
 
 def handoff_kernel(
@@ -31,7 +216,13 @@
     state_ref,
     message_ref,
     edge_ref,
-    incoming_ref,
+    live_ref,
+    head_gain_ref,
+    local_hbm,
+    query_hbm,
+    gate_hbm,
+    out_hbm,
+    mixed_ref,
     owned_ref,
     owned_edge_ref,
     parts,
@@ -55,6 +246,21 @@
     recv_edge,
     send_picked,
     recv_picked,
+    local,
+    query,
+    gate,
+    w_out,
+    to_far,
+    to_left,
+    to_right,
+    relay_right,
+    relay_left,
+    sum_right,
+    sum_left,
+    load_sem,
+    send_sum,
+    recv_relay,
+    recv_sum,
 ):
     me = lax.axis_index("seq")
     lane_blocks = state_ref.shape[1] // 128
@@ -72,14 +278,27 @@
         pl.semaphore_signal(barrier, inc=1, device_id={"seq": peer}, device_id_type=MESH)
         return 0
 
+    loads = [
+        pltpu.make_async_copy(local_hbm, local, load_sem.at[0]),
+        pltpu.make_async_copy(query_hbm, query, load_sem.at[1]),
+        pltpu.make_async_copy(gate_hbm, gate, load_sem.at[2]),
+        pltpu.make_async_copy(out_hbm, w_out, load_sem.at[3]),
+    ]
+    for load in loads:
+        load.start()
+    x, right, left, far = neighbours()
     lax.fori_loop(1, n, greet, 0)
-    pl.semaphore_wait(barrier, n - 1)
+    for peer in (right, left):
+        pl.semaphore_signal(barrier, inc=1, device_id={"tensor": peer}, device_id_type=MESH)
+    pl.semaphore_wait(barrier, n + 1)
 
     my_block = block_of(me)
+    key_row = (me // lane_blocks) * rows
+    wide = max(rows, 128)
 
     def message_to(peer):
         return pltpu.make_async_remote_copy(
-            src_ref=message_ref,
+            src_ref=message_ref.at[((peer // lane_blocks) * rows) // wide],
             dst_ref=messages.at[me],
             send_sem=send_message.at[peer],
             recv_sem=recv_message.at[me],
@@ -160,7 +379,7 @@
 
     lax.fori_loop(1, n, send_first, 0)
     parts[me] = state_ref[my_block]
-    messages[me] = message_ref[...]
+    messages[me] = message_ref[key_row // wide]
 
     def arrived(make, ref_of, sem):
         def wait(step, _):
@@ -183,7 +402,7 @@
     def pick_edges(step, _):
         other = lax.rem(member + step, group)
         for slot in range(2):
-            wanted = messages[first_of_group + other, :, pl.ds(256 + 128 * slot, 128)]
+            wanted = messages[first_of_group + other, :, pl.ds(wide + 128 * slot, 128)]
             picked = jnp.zeros(edge_ref.shape, jnp.float32)
             for upper in range(levels):
                 ended = end_ref[upper * group + member].astype(jnp.float32)
@@ -200,7 +419,6 @@
     owned_edges[member] = picked_edges[member]
     arrived(None, lambda peer: parts.at[peer], recv_part)
 
-    key_row = (me // lane_blocks) * rows
     tall = min(rows, 128)
     lanes = lax.broadcasted_iota(jnp.int32, (tall, 128), 1)
     sublanes = lax.broadcasted_iota(jnp.int32, (tall, 128), 0)
@@ -209,8 +427,7 @@
     def decay_column(index):
         columns = []
         for part in range(rows // tall):
-            first = pl.multiple_of((key_row // 128 + part) * 128, 128)
-            row = messages[index, :, pl.ds(first, 128)]
+            row = messages[index, :, pl.ds(part * 128, 128)]
             columns.append(
                 jnp.sum(jnp.where(lanes == offset, row, 0.0), axis=1, keepdims=True)
             )
@@ -238,7 +455,7 @@
     def hand(step, _):
         peer = lax.rem(me + step, n)
         for slot in range(2):
-            wanted = messages[peer, :, pl.ds(256 + 128 * slot, 128)]
+            wanted = messages[peer, :, pl.ds(wide + 128 * slot, 128)]
             picked = zero
             for p, final in enumerate(finals):
                 picked = jnp.where(wanted == float(p), final, picked)
@@ -255,7 +472,78 @@
     owned[(slice(None),) + my_block] = handed[me]
 
     arrived(None, lambda peer: incoming.at[block_of(peer)], recv_back)
-    incoming_ref[...] = incoming[...]
+    for load in loads:
+        load.wait()
+    share = mixed_ref.shape[0]
+    half = share // 2
+    lower, upper = pl.ds(0, half), pl.ds(half, half)
+
+    def partial_of(quarter):
+        here = pl.ds(pl.multiple_of(quarter * share, share), share)
+        skipped = pl.ds(pl.multiple_of(quarter * share + HALO, HALO), share)
+        attended = local[here, :] + jnp.dot(
+            query[here, :], incoming[...], preferred_element_type=jnp.float32
+        )
+        mean_square = jnp.mean(attended * attended, axis=1, keepdims=True)
+        gate_values = gate[skipped, :].astype(jnp.float32)
+        gated = (
+            attended
+            * lax.rsqrt(mean_square + EPS_HEAD)
+            * head_gain_ref[...]
+            * (gate_values * jax.nn.sigmoid(gate_values))
+        ).astype(jnp.bfloat16)
+        return jnp.dot(gated, w_out[...], preferred_element_type=jnp.float32).astype(jnp.bfloat16)
+
+    def move(src, dst, to, index, recv):
+        return pltpu.make_async_remote_copy(
+            src_ref=src,
+            dst_ref=dst,
+            send_sem=send_sum.at[index],
+            recv_sem=recv,
+            device_id={"tensor": to},
+            device_id_type=MESH,
+        )
+
+    moves = [
+        move(to_far.at[lower], relay_right, left, 0, recv_relay.at[0]),
+        move(to_far.at[upper], relay_left, right, 1, recv_relay.at[1]),
+        move(to_left.at[upper], sum_right.at[upper], left, 2, recv_sum.at[0]),
+        move(to_right.at[lower], sum_left.at[lower], right, 3, recv_sum.at[1]),
+        move(to_left.at[lower], sum_right.at[lower], left, 4, recv_sum.at[2]),
+        move(to_right.at[upper], sum_left.at[upper], right, 5, recv_sum.at[3]),
+    ]
+    to_far[...] = partial_of(far)
+    moves[0].start()
+    moves[1].start()
+    to_left[...] = partial_of(left)
+    moves[2].start()
+    to_right[...] = partial_of(right)
+    moves[3].start()
+    moves[0].wait_recv()
+    to_left[lower, :] = (
+        to_left[lower, :].astype(jnp.float32) + relay_right[...].astype(jnp.float32)
+    ).astype(jnp.bfloat16)
+    moves[4].start()
+    moves[1].wait_recv()
+    to_right[upper, :] = (
+        to_right[upper, :].astype(jnp.float32) + relay_left[...].astype(jnp.float32)
+    ).astype(jnp.bfloat16)
+    moves[5].start()
+    to_far_done = (moves[0], moves[1])
+    for copy in to_far_done:
+        copy.wait_send()
+    to_far[...] = partial_of(x)
+    for copy in moves[2:]:
+        copy.wait_recv()
+    summed = (
+        to_far[...].astype(jnp.float32)
+        + sum_right[...].astype(jnp.float32)
+        + sum_left[...].astype(jnp.float32)
+    )
+    row_of = x * share + lax.broadcasted_iota(jnp.int32, (share, 1), 0)
+    mixed_ref[...] = jnp.where(row_of < live_ref[0], summed, 0.0).astype(jnp.bfloat16)
+    for copy in moves[2:]:
+        copy.wait_send()
     arrived(None, lambda peer: owned.at[(slice(None),) + block_of(peer)], recv_handed)
     owned_ref[...] = owned[...].astype(jnp.float32)
 
@@ -284,29 +572,50 @@
     lax.fori_loop(1, n, drain, 0)
 
 
-def handoff(state, decay, edge, wanted, starts_here, ends_here):
+def handoff(
+    state,
+    decay,
+    edge,
+    wanted,
+    starts_here,
+    ends_here,
+    live_rows,
+    head_gain,
+    local_out,
+    query_decayed,
+    gate_values,
+    w_out,
+):
     n = lax.axis_size("seq")
     group = 8 if n % 8 == 0 else n // 2
     keys, values = state.shape
     rows = keys * (values // 128) // n
+    share = local_out.shape[0] // lax.axis_size("tensor")
+    wide = max(rows, 128)
+    pieces = keys // wide
     message = jnp.concatenate(
-        [decay, jnp.broadcast_to(wanted.astype(jnp.float32)[:, None], (2, 128)).reshape(1, 256)],
-        axis=1,
+        [
+            decay.reshape(pieces, 1, wide),
+            jnp.broadcast_to(
+                wanted.astype(jnp.float32)[None, :, None], (pieces, 2, 128)
+            ).reshape(pieces, 1, 256),
+        ],
+        axis=2,
     )
     vmem = pl.BlockSpec(memory_space=pltpu.VMEM)
     smem = pl.BlockSpec(memory_space=pltpu.SMEM)
     return pl.pallas_call(
         functools.partial(handoff_kernel, n, group, rows),
         out_shape=(
-            jax.ShapeDtypeStruct((keys, values), jnp.bfloat16),
+            jax.ShapeDtypeStruct((share, w_out.shape[1]), jnp.bfloat16),
             jax.ShapeDtypeStruct((2, keys, values), jnp.float32),
             jax.ShapeDtypeStruct((2,) + edge.shape, jnp.bfloat16),
         ),
-        in_specs=[smem, smem, vmem, vmem, vmem],
+        in_specs=[smem, smem, vmem, vmem, vmem, smem, vmem] + [pl.BlockSpec(memory_space=pl.ANY)] * 4,
         out_specs=(vmem, vmem, vmem),
         scratch_shapes=[
             pltpu.VMEM((n, rows, 128), jnp.bfloat16),
-            pltpu.VMEM((n, 1, 512), jnp.float32),
+            pltpu.VMEM((n, 1, wide + 256), jnp.float32),
             pltpu.VMEM((n, rows, 128), jnp.bfloat16),
             pltpu.VMEM((n, 2, rows, 128), jnp.bfloat16),
             pltpu.VMEM((keys, values), jnp.bfloat16),
@@ -321,10 +630,39 @@
             pltpu.SemaphoreType.DMA((n // group,)),
             pltpu.SemaphoreType.DMA((group,)),
             pltpu.SemaphoreType.DMA((group,)),
+            pltpu.VMEM(local_out.shape, jnp.float32),
+            pltpu.VMEM(query_decayed.shape, jnp.bfloat16),
+            pltpu.VMEM(gate_values.shape, jnp.bfloat16),
+            pltpu.VMEM(w_out.shape, jnp.bfloat16),
+            pltpu.VMEM((share, w_out.shape[1]), jnp.bfloat16),
+            pltpu.VMEM((share, w_out.shape[1]), jnp.bfloat16),
+            pltpu.VMEM((share, w_out.shape[1]), jnp.bfloat16),
+            pltpu.VMEM((share // 2, w_out.shape[1]), jnp.bfloat16),
+            pltpu.VMEM((share // 2, w_out.shape[1]), jnp.bfloat16),
+            pltpu.VMEM((share, w_out.shape[1]), jnp.bfloat16),
+            pltpu.VMEM((share, w_out.shape[1]), jnp.bfloat16),
+            pltpu.SemaphoreType.DMA((4,)),
+            pltpu.SemaphoreType.DMA((6,)),
+            pltpu.SemaphoreType.DMA((2,)),
+            pltpu.SemaphoreType.DMA((4,)),
         ],
-        compiler_params=pltpu.CompilerParams(collective_id=0, has_side_effects=True),
+        compiler_params=pltpu.CompilerParams(
+            collective_id=0, has_side_effects=True, vmem_limit_bytes=48 * 1024 * 1024
+        ),
         name="state_handoff",
-    )(starts_here, ends_here, state, message, edge)
+    )(
+        starts_here,
+        ends_here,
+        state,
+        message,
+        edge,
+        live_rows.reshape(1),
+        head_gain.reshape(1, -1),
+        local_out,
+        query_decayed,
+        gate_values,
+        w_out,
+    )
 
 
 def local_kernel(
@@ -372,7 +710,7 @@
         key = jnp.where(valid, activated[:, keys : 2 * keys].astype(jnp.float32), 0.0)
         value = activated[:, 2 * keys :]
         logits = contract(
-            low_rank_ref[here, :], gate_up_ref[...], ((1,), (0,)), EXACT_MATMUL
+            low_rank_ref[pl.ds(base + halo, STRETCH), :], gate_up_ref[...], ((1,), (0,)), EXACT_MATMUL
         ) + gate_bias_ref[...]
         log_decay = (jnp.minimum(logits, 0.0) - jnp.log1p(jnp.exp(-jnp.abs(logits)))) / 16.0
         log_decay = jnp.where(valid, log_decay, 0.0)
@@ -426,7 +764,7 @@
 
 
 def local_blocks(live_rows, projected, low_rank, gate_up, gate_bias, conv_weight, values):
-    rows = low_rank.shape[0]
+    rows = low_rank.shape[0] - HALO
     keys = gate_up.shape[1]
     vmem = pl.BlockSpec(memory_space=pltpu.VMEM)
     smem = pl.BlockSpec(memory_space=pltpu.SMEM)
@@ -482,32 +820,14 @@
     is_start = seq_index == first_dev
     is_last = seq_index == last_dev
     live_rows = jnp.where(is_last, jnp.sum(jnp.where(picked, fills, 0)), row_count)
-    valid = jnp.arange(row_count, dtype=jnp.int32) < live_rows
-    value_entries = tokens.astype(jnp.float32)
-    squares = lax.psum(jnp.sum(value_entries * value_entries, axis=1), "tensor")
-    inverse = lax.rsqrt(squares / model_width + EPS_IN)
     flat_qkv = w_qkv.reshape(model_width, local_heads * width_qkv)
-    normed = (
-        lax.all_gather(tokens, "tensor", axis=1, tiled=True).astype(jnp.float32)
-        * inverse[:, None]
-        * norm_gain[None, :]
-    ).astype(jnp.bfloat16)
-    qkv_sum = jnp.dot(normed, flat_qkv, preferred_element_type=jnp.float32)
-    gate_sum = jnp.dot(normed, w_gate_out, preferred_element_type=jnp.float32)
-    low_rank = jnp.dot(normed, gate_down, preferred_element_type=jnp.float32)
-    projected = qkv_sum.astype(jnp.bfloat16).reshape(row_count, local_heads, width_qkv)
-    gate_rounded = lax.optimization_barrier(gate_sum.astype(jnp.bfloat16))
-    gate_values = gate_rounded.astype(jnp.float32).reshape(row_count, local_heads, value_width)
-    tail_rows = projected[row_count - taps + 1 :]
-    previous = from_behind(tail_rows, "seq", 1)
-    previous = jnp.where(is_start, jnp.zeros_like(previous), previous)
-    halo = 16
-    front = jnp.zeros((halo - taps + 1, width_qkv), jnp.bfloat16)
-    extended = jnp.concatenate([front, previous[:, 0], projected[:, 0]], axis=0)
+    extended, gate_values, low_rank = project(
+        is_start.astype(jnp.int32), tokens, norm_gain, flat_qkv, w_gate_out, gate_down
+    )
     local_out, query_decayed, local_state, decay = local_blocks(
         live_rows, extended, low_rank, gate_up[:, 0], gate_bias, conv_weight[:, 0], value_width
     )
-    edge_rows = lax.dynamic_slice_in_dim(extended, live_rows + halo - taps + 1, taps - 1, 0)
+    edge_rows = lax.dynamic_slice_in_dim(extended, live_rows + HALO - taps + 1, taps - 1, 0)
     edge = jnp.pad(edge_rows.reshape(-1, 128), ((0, 8), (0, 0)))
     devices = jnp.arange(lax.axis_size("seq"), dtype=jnp.int32)
     starts_here = jnp.any(devices[:, None] == starts[None, :], axis=1).astype(jnp.int32)
@@ -519,32 +839,24 @@
         ),
         axis=1,
     ) - 2
-    incoming, owner_state, owned_edge = handoff(
-        local_state, decay, edge, request_prompt, starts_here, ends_here
+    mixed, owner_state, owned_edge = handoff(
+        local_state,
+        decay,
+        edge,
+        request_prompt,
+        starts_here,
+        ends_here,
+        live_rows,
+        head_gain,
+        local_out,
+        query_decayed,
+        gate_values,
+        w_out,
     )
     owner_state = owner_state[:, None]
     owner_edge = owned_edge[:, : edge.shape[0] - 8].reshape(
         slot_count, taps - 1, local_heads, width_qkv
     )
-    attended = local_out + jnp.dot(query_decayed, incoming, preferred_element_type=jnp.float32)
-    attended = attended.reshape(row_count, local_heads, value_width)
-    mean_square = jnp.mean(attended * attended, axis=2, keepdims=True)
-    gated = (
-        attended
-        * lax.rsqrt(mean_square + EPS_HEAD)
-        * head_gain[None, None, :]
-        * jax.nn.silu(gate_values)
-    ).astype(jnp.bfloat16)
-    gated = gated.reshape(row_count, local_heads * value_width)
-    share = row_count // lax.axis_size("tensor")
-    summed = lax.psum_scatter(
-        jnp.dot(gated, w_out, preferred_element_type=jnp.float32).astype(jnp.bfloat16),
-        "tensor",
-        scatter_dimension=0,
-        tiled=True,
-    ).astype(jnp.float32)
-    own_rows = lax.axis_index("tensor") * share + jnp.arange(share, dtype=jnp.int32)
-    mixed = jnp.where((own_rows < live_rows)[:, None], summed, 0.0).astype(jnp.bfloat16)
     return (mixed, owner_state, owner_edge)
 
 

time: 172 us -> 131 us (0.76)
  the two profiles are of different devices: /device:TPU:1 before, /device:TPU:241 now
where the time goes in v3:
time: 131 us; the launch traced here: 130 us
  Pallas kernels  104 us (79%)
  local copies, waits for them, and re-layouts  18.1 us (14%)
  other arithmetic  5.06 us (4%)
  between operations  2.71 us (2%)
    pallas_call x1, Pallas kernels, handoff(): pl.pallas_call(functools.partial(handoff_kernel, n, group, rows), out_sha...  65.9 us
    pallas_call x1, Pallas kernels, project(): pl.pallas_call(project_kernel, out_shape=(jax.ShapeDtypeStruct((tall, w_q...  25.4 us
    unnamed x32, local copies, waits for them, and re-layouts  18 us
    pallas_call x1, Pallas kernels, local_blocks(): pl.pallas_call(local_kernel, out_shape=(jax.ShapeDtypeStruct((rows, value...  12.7 us

profile of v3, /device:TPU:241, one launch (start us, length us, event | category | flops | bytes accessed | tf_op | source)
XLA Modules:
  0.0 130.0 jit_solution(17326748555955326213)
XLA Ops:
  0.6 0.8 reduce-window.7
  1.5 0.6 fusion.1
  2.1 0.7 convert_element_type.14
  2.8 0.1 broadcast_bitcast_fusion
  2.8 2.1 %select_reduce_fusion.3 = (s32[]{:T(128)}, s32[3]{0:T(128)S(1)}, s32[]{:T(128)}, s32[3]{0:T(128)S(1)}, s32[]{:T(128)}) fusion(s32[]{:T(128)} %fusion.1, s32[3,1]{0,1:T(1,128)S(1)} %reduce-window.7, s32[3]{0:T(128)} %param.23, s32[3]{0:T(128)} %param.24), kind=kLoop, calls=%fused_computation.13 | loop fusion | flops 24 | bytes 76 | tf_op jit(solution)/shard_map/reduce_sum | solution.py:819
  6.9 0.1 select_reduce_fusion
  7.0 0.1 fusion
  7.1 1.3 %copy.30 = f32[16,1,256]{2,0,1:T(8,128)} copy(f32[16,1,256]{2,1,0:T(1,128)} %param.18) | data formatting | bytes 32768
  8.4 1.3 %copy.29 = f32[4,1,1024]{2,0,1:T(4,128)} copy(f32[4,1,1024]{2,1,0:T(1,128)} %param.20) | data formatting | bytes 32768
  9.7 1.1 copy.22.down_ref
  10.8 0.0 copy-start
  10.9 1.6 %copy-done = bf16[2048,512]{1,0:T(8,128)(2,1)S(1)} copy-done((bf16[2048,512]{1,0:T(8,128)(2,1)S(1)}, bf16[2048,512]{1,0:T(8,128)(2,1)}, u32[]{:S(2)}) %copy-start) | copy-done | bytes 2097176
  12.4 0.0 copy-start.6
  12.4 1.0 copy-done.6
  13.5 0.0 copy-start.11
  13.5 0.7 copy-done.11
  14.2 0.0 copy-start.1
  14.2 0.0 copy-start.12
  14.2 25.4 %gather_project.1 = (bf16[528,1024]{1,0:T(8,128)(2,1)S(1)}, bf16[528,512]{1,0:T(8,128)(2,1)S(1)}, f32[528,16]{1,0:T(8,128)S(1)}) custom-call(s32[1]{0:T(128)} %bitcast.3.start_ref, bf16[512,512]{1,0:T(8,128)(2,1)S(1)} %copy-done.6, f32[1,2048]{1,0:T(1,128)S(1)} %bitcast.26, bf16[2048,1024]{1,0:T(8,128)(2,1)} %bitcast.28, bf16[2048,512]{1,0:T(8,128)(2,1)S(1)} %copy-done, ...), custom_call_target="tpu_custom_call" | custom-call | tf_op jit(solution)/shard_map/gather_project/pallas_call | solution.py:185
  39.6 0.0 copy-start.4
  39.6 0.8 copy-done.4
  40.4 0.0 copy-start.8
  40.4 0.7 copy-done.8
  41.1 0.0 copy-start.2
  41.2 1.0 copy-done.2
  42.2 12.7 %local_blocks.1 = (f32[512,512]{1,0:T(8,128)}, bf16[512,256]{1,0:T(8,128)(2,1)}, bf16[256,512]{1,0:T(8,128)(2,1)}, f32[1,256]{1,0:T(1,128)}) custom-call(s32[1]{0:T(128)} %bitcast.2.live_ref, bf16[528,1024]{1,0:T(8,128)(2,1)} %copy-done.2, f32[528,16]{1,0:T(8,128)} %copy-done.8, f32[16,256]{1,0:T(8,128)} %bitcast.29, f32[1,256]{1,0:T(1,128)} %gate_bias_ref.1, ...), custom_call_target="tpu_custom_call" | custom-call | tf_op jit(solution)/shard_map/local_blocks/pallas_call | solution.py:771
  54.9 0.7 pad_maximum_fusion.message_ref
  55.6 0.0 copy-done.1
  55.6 0.0 copy-done.12
  55.6 0.0 copy-start.3
  55.6 1.2 copy-done.3
  56.8 0.0 copy-start.5
  56.8 1.0 copy-done.5
  57.9 0.0 copy-start.9
  57.9 0.9 copy-done.9
  58.8 0.0 copy-start.10
  58.8 0.9 copy-done.10
  59.8 65.9 %state_handoff.1 = (bf16[128,2048]{1,0:T(8,128)(2,1)S(1)}, f32[2,256,512]{2,1,0:T(8,128)S(1)}, bf16[2,32,128]{2,1,0:T(8,128)(2,1)S(1)}) custom-call(s32[64]{0:T(128)S(1)} %convert_element_type.12.start_ref, s32[64]{0:T(128)S(1)} %broadcast_add_fusion.end_ref, bf16[256,512]{1,0:T(8,128)(2,1)S(1)} %copy-done.10, f32[2,1,384]{2,1,0:T(1,128)S(1)} %pad_maximum_fusion.message_ref, ...), custom_call_target="tpu_custom_call" | custom-call | tf_op jit(solution)/shard_map/state_handoff/pallas_call | solution.py:607
  125.7 0.0 copy-start.7
  125.7 0.8 copy-done.7
  126.5 0.6 copy.24
  127.1 1.9 %copy.33 = bf16[128,2048]{1,0:T(8,128)(2,1)} copy(bf16[128,2048]{1,0:T(8,128)(2,1)} %copy-done.7) | data formatting | bytes 1048576
  129.0 1.0 copy.34
  (9 shorter events, 0.1 us)
Async XLA Ops:
  10.8 1.6 %copy-start = (bf16[2048,512]{1,0:T(8,128)(2,1)S(1)}, bf16[2048,512]{1,0:T(8,128)(2,1)}, u32[]{:S(2)}) copy-start(bf16[2048,512]{1,0:T(8,128)(2,1)} %gate_hbm.1) | copy-start | bytes 6291460
  12.4 1.0 copy-start.6
  13.5 0.7 copy-start.11
  14.2 41.4 %copy-start.1 = (bf16[512,2048]{1,0:T(8,128)(2,1)S(1)}, bf16[512,2048]{1,0:T(8,128)(2,1)}, u32[]{:S(2)}) copy-start(bf16[512,2048]{1,0:T(8,128)(2,1)} %out_hbm.1) | copy-start | bytes 6291460
  14.2 41.4 %copy-start.12 = (f32[512]{0:T(512)S(1)}, f32[512]{0:T(512)}, u32[]{:S(2)}) copy-start(f32[512]{0:T(512)} %param.21) | copy-start | bytes 6148
  39.6 0.8 copy-start.4
  40.4 0.7 copy-start.8
  41.1 1.0 copy-start.2
  55.6 1.2 copy-start.3
  56.8 1.0 copy-start.5
  57.9 0.9 copy-start.9
  58.8 0.9 copy-start.10
  125.7 0.8 copy-start.7

commit v4 on v3

v4 whole, which is shorter than its diff:
```python
import functools

import jax
import jax.numpy as jnp
from jax import lax
from jax.experimental import pallas as pl
from jax.experimental.pallas import tpu as pltpu
from jax.sharding import PartitionSpec as P

STRETCH = 64


EPS_IN = 1e-06
EPS_HEAD = 1e-05
EXACT_MATMUL = lax.Precision.HIGHEST
MESH = pl.DeviceIdType.MESH


HALO = 16
CHUNKS = ((16, 96, 176), (176, 272, 352), (352, 448, 528))


def neighbours():
    n = lax.axis_size("tensor")
    x = lax.axis_index("tensor")
    return x, lax.rem(x + 1, n), lax.rem(x + n - 1, n), lax.rem(x + 2, n)


def prompt_edges(spans_ref):
    ends = []
    for p in range(spans_ref.shape[0]):
        ends.append(spans_ref[p] + ends[-1] if ends else spans_ref[p])
    return ends


def starts_prompt(index, ends):
    flag = index == 0
    for end in ends[:-1]:
        flag = flag | (index == end)
    return flag


def live_rows_of(index, ends, fills_ref, rows):
    live = rows
    for p, end in enumerate(ends):
        live = jnp.where(index == end - 1, fills_ref[p], live)
    return live


def project_kernel(
    spans_ref,
    tokens_ref,
    gain_hbm,
    qkv_hbm,
    gate_hbm,
    down_hbm,
    projected_ref,
    gate_ref,
    low_rank_ref,
    gathered,
    normed,
    qkv,
    gate,
    gain_ref,
    down_ref,
    load_sem,
    send_right,
    send_left,
    from_left,
    from_right,
    pass_right,
    pass_left,
    far_left,
    far_right,
    send_halo,
    recv_halo,
):
    n = lax.axis_size("seq")
    peers = lax.axis_size("tensor")
    me = lax.axis_index("seq")
    x, right, left, far = neighbours()
    after, before = lax.rem(me + 1, n), lax.rem(me + n - 1, n)
    width = tokens_ref.shape[1]
    loads = [
        pltpu.make_async_copy(qkv_hbm, qkv, load_sem.at[0]),
        pltpu.make_async_copy(gate_hbm, gate, load_sem.at[1]),
        pltpu.make_async_copy(gain_hbm, gain_ref, load_sem.at[2]),
        pltpu.make_async_copy(down_hbm, down_ref, load_sem.at[3]),
        pltpu.make_async_copy(
            tokens_ref, gathered.at[x, pl.ds(HALO, tokens_ref.shape[0])], load_sem.at[4]
        ),
    ]
    for load in loads:
        load.start()

    barrier = pltpu.get_barrier_semaphore()
    for peer in (right, left):
        pl.semaphore_signal(barrier, inc=1, device_id={"tensor": peer}, device_id_type=MESH)
    for peer in range(peers):
        pl.semaphore_signal(
            barrier, inc=1, device_id={"seq": before, "tensor": peer}, device_id_type=MESH
        )
    pl.semaphore_wait(barrier, 2 + peers)

    def own(chunk, to, send, recv):
        first, _, last = CHUNKS[chunk]
        return pltpu.make_async_remote_copy(
            src_ref=tokens_ref.at[pl.ds(first - HALO, last - first)],
            dst_ref=gathered.at[x, pl.ds(first, last - first)],
            send_sem=send.at[chunk],
            recv_sem=recv.at[chunk],
            device_id={"tensor": to},
            device_id_type=MESH,
        )

    def passed(chunk, owner, to, upper, send, recv):
        first, middle, last = CHUNKS[chunk]
        first, last = (middle, last) if upper else (first, middle)
        ref = gathered.at[owner, pl.ds(first, last - first)]
        return pltpu.make_async_remote_copy(
            src_ref=ref,
            dst_ref=ref,
            send_sem=send.at[chunk],
            recv_sem=recv.at[chunk],
            device_id={"tensor": to},
            device_id_type=MESH,
        )

    def landed(owner, first, last, sem):
        ref = gathered.at[owner, pl.ds(first, last - first)]
        pltpu.make_async_copy(ref, ref, sem).wait()

    halos = []
    for peer in range(peers):
        halos.append(
            pltpu.make_async_remote_copy(
                src_ref=tokens_ref.at[pl.ds(tokens_ref.shape[0] - HALO, HALO)],
                dst_ref=gathered.at[x, pl.ds(0, HALO)],
                send_sem=send_halo.at[peer],
                recv_sem=recv_halo.at[x],
                device_id={"seq": after, "tensor": peer},
                device_id_type=MESH,
            )
        )
    count = len(CHUNKS)
    rights = [own(c, right, send_right, from_left) for c in range(count)]
    lefts = [own(c, left, send_left, from_right) for c in range(count)]
    onward_right = [passed(c, left, right, False, pass_right, far_left) for c in range(count)]
    onward_left = [passed(c, right, left, True, pass_left, far_right) for c in range(count)]
    for copy in (rights[0], lefts[0], *halos, rights[1], lefts[1]):
        copy.start()

    def compute(chunk):
        first = 0 if chunk == 0 else CHUNKS[chunk][0]
        last = CHUNKS[chunk][2]
        here = pl.ds(first, last - first)
        squares = jnp.zeros((last - first, 1), jnp.float32)
        for owner in range(peers):
            piece = gathered[owner, here].astype(jnp.float32)
            squares = squares + jnp.sum(piece * piece, axis=1, keepdims=True)
        inverse = lax.rsqrt(squares / (width * peers) + EPS_IN)
        for owner in range(peers):
            lanes = pl.ds(owner * width, width)
            piece = gathered[owner, here].astype(jnp.float32)
            normed[:, lanes] = (piece * inverse * gain_ref[:, lanes]).astype(jnp.bfloat16)
        rows = normed[...]
        made = jnp.dot(rows, qkv[...], preferred_element_type=jnp.float32)
        if chunk == 0:
            row_of = lax.broadcasted_iota(jnp.int32, (last - first, 1), 0)
            made = jnp.where((row_of < HALO) & starts_prompt(me, prompt_edges(spans_ref)), 0.0, made)
        projected_ref[here, :] = made.astype(jnp.bfloat16)
        gate_ref[here, :] = jnp.dot(
            rows, gate[...], preferred_element_type=jnp.float32
        ).astype(jnp.bfloat16)
        low_rank_ref[here, :] = lax.dot_general(
            rows,
            down_ref[...],
            (((1,), (1,)), ((), ())),
            preferred_element_type=jnp.float32,
        )

    def arrive_and_compute(chunk):
        first, middle, last = CHUNKS[chunk]
        landed(far, first, middle, far_left.at[chunk])
        landed(far, middle, last, far_right.at[chunk])
        if chunk == 0:
            for load in loads:
                load.wait()
            for peer in range(peers):
                landed(peer, 0, HALO, recv_halo.at[peer])
        compute(chunk)

    for chunk in range(count):
        first, middle, last = CHUNKS[chunk]
        landed(left, first, last, from_left.at[chunk])
        onward_right[chunk].start()
        landed(right, first, last, from_right.at[chunk])
        onward_left[chunk].start()
        if chunk + 2 < count:
            rights[chunk + 2].start()
            lefts[chunk + 2].start()
        if chunk:
            arrive_and_compute(chunk - 1)
    arrive_and_compute(count - 1)
    for copy in (*rights, *lefts, *onward_right, *onward_left, *halos):
        copy.wait_send()


def project(spans, tokens, norm_gain, w_qkv, w_gate_out, gate_down):
    rows, width = tokens.shape
    vmem = pl.BlockSpec(memory_space=pltpu.VMEM)
    smem = pl.BlockSpec(memory_space=pltpu.SMEM)
    hbm = pl.BlockSpec(memory_space=pltpu.HBM)
    peers = lax.axis_size("tensor")
    tall = rows + HALO
    count = len(CHUNKS)
    return pl.pallas_call(
        project_kernel,
        out_shape=(
            jax.ShapeDtypeStruct((tall, w_qkv.shape[1]), jnp.bfloat16),
            jax.ShapeDtypeStruct((tall, w_gate_out.shape[1]), jnp.bfloat16),
            jax.ShapeDtypeStruct((tall, gate_down.shape[1]), jnp.float32),
        ),
        in_specs=[smem] + [hbm] * 5,
        out_specs=(vmem,) * 3,
        scratch_shapes=[
            pltpu.VMEM((peers, tall, width), jnp.bfloat16),
            pltpu.VMEM((tall // count, width * peers), jnp.bfloat16),
            pltpu.VMEM(w_qkv.shape, jnp.bfloat16),
            pltpu.VMEM(w_gate_out.shape, jnp.bfloat16),
            pltpu.VMEM((1, width * peers), jnp.float32),
            pltpu.VMEM((gate_down.shape[1], width * peers), jnp.bfloat16),
            pltpu.SemaphoreType.DMA((5,)),
        ]
        + [pltpu.SemaphoreType.DMA((count,))] * 8
        + [pltpu.SemaphoreType.DMA((peers,))] * 2,
        compiler_params=pltpu.CompilerParams(
            collective_id=1, has_side_effects=True, vmem_limit_bytes=20 * 1024 * 1024
        ),
        name="gather_project",
    )(
        spans,
        *(
            pltpu.with_memory_space_constraint(array, pltpu.HBM)
            for array in (tokens, norm_gain.reshape(1, -1), w_qkv, w_gate_out, gate_down.T)
        ),
    )


def handoff_kernel(
    n,
    group,
    rows,
    spans_ref,
    fills_ref,
    request_ref,
    state_ref,
    decay_ref,
    edge_ref,
    head_gain_ref,
    local,
    query,
    gate,
    w_out,
    mixed_ref,
    owned_ref,
    owned_edge_ref,
    message,
    parts,
    messages,
    decays,
    back,
    incoming,
    finals,
    all_finals,
    handed,
    owned,
    edges,
    picked_edges,
    owned_edges,
    to_far,
    to_left,
    to_right,
    relay_right,
    relay_left,
    sum_right,
    sum_left,
    send_sem,
    recv_sem,
    send_sum,
    recv_relay,
    recv_sum,
):
    me = lax.axis_index("seq")
    lane_blocks = state_ref.shape[1] // 128
    slots = request_ref.shape[0]
    ends = prompt_edges(spans_ref)
    wide = max(rows, 128)

    def block_of(index):
        return (
            pl.ds(pl.multiple_of(lax.div(index, lane_blocks) * rows, rows), rows),
            pl.ds(pl.multiple_of(lax.rem(index, lane_blocks) * 128, 128), 128),
        )

    my_block = block_of(me)
    key_row = lax.div(me, lane_blocks) * rows
    level, member = lax.div(me, group), lax.rem(me, group)
    levels = n // group
    first_of_group = level * group
    x, right, left, far = neighbours()

    def around(count, own, action):
        inner = max(k for k in range(1, 10) if (count - 1) % k == 0)

        def run(outer, _):
            for k in range(inner):
                action(lax.rem(own + (outer * inner + k + 1), count))
            return 0

        lax.fori_loop(0, (count - 1) // inner, run, 0)

    def greet(peer):
        pl.semaphore_signal(barrier, inc=1, device_id={"seq": peer}, device_id_type=MESH)

    barrier = pltpu.get_barrier_semaphore()
    around(n, me, greet)
    for peer in (right, left):
        pl.semaphore_signal(barrier, inc=1, device_id={"tensor": peer}, device_id_type=MESH)
    for piece in range(message.shape[0]):
        message[piece, :, :wide] = decay_ref[:, piece * wide : (piece + 1) * wide]
        for slot in range(slots):
            wanted = request_ref[slot].astype(jnp.float32)
            message[piece, :, wide + 128 * slot : wide + 128 * (slot + 1)] = jnp.full(
                (1, 128), wanted, jnp.float32
            )
    pl.semaphore_wait(barrier, n + 1)

    def to_seq(src, dst, peer, index):
        return pltpu.make_async_remote_copy(
            src_ref=src,
            dst_ref=dst,
            send_sem=send_sem.at[index],
            recv_sem=recv_sem.at[index],
            device_id={"seq": peer},
            device_id_type=MESH,
        )

    def message_to(peer):
        piece = lax.div(lax.div(peer, lane_blocks) * rows, wide)
        return to_seq(message.at[piece], messages.at[me], peer, 0)

    def part_to(peer):
        return to_seq(state_ref.at[block_of(peer)], parts.at[me], peer, 1)

    def edge_to(other):
        return to_seq(edge_ref, edges.at[level], other * group + member, 2)

    def picked_to(other):
        return to_seq(
            picked_edges.at[other], owned_edges.at[member], first_of_group + other, 3
        )

    def back_to(peer):
        return to_seq(back.at[peer], incoming.at[my_block], peer, 4)

    def finals_to(other):
        return to_seq(finals, all_finals.at[level], other * group + member, 5)

    mine = (
        slice(None),
        slice(None),
        lax.div(member, lane_blocks),
        slice(None),
        pl.ds(pl.multiple_of(lax.rem(member, lane_blocks) * 128, 128), 128),
    )

    def handed_to(other):
        return to_seq(handed.at[other], owned.at[mine], first_of_group + other, 6)

    def whole(ref, count, sem):
        few = ref.at[pl.ds(0, count)]
        pltpu.make_async_copy(few, few, sem).wait()

    def send_first(peer):
        message_to(peer).start()
        part_to(peer).start()

    around(n, me, send_first)
    around(levels, level, lambda other: edge_to(other).start()) if levels > 1 else None
    parts[me] = state_ref[my_block]
    messages[me] = message[lax.div(key_row, wide)]
    edges[level] = edge_ref[...]
    whole(messages, n - 1, recv_sem.at[0])

    tall = min(rows, 128)
    lanes = lax.broadcasted_iota(jnp.int32, (tall, 128), 1)
    offset = lax.rem(key_row, 128) + lax.broadcasted_iota(jnp.int32, (tall, 128), 0)
    zero = jnp.zeros((rows, 128), jnp.float32)
    step = 8 if n % 8 == 0 else n

    def spread(outer, _):
        for k in range(step):
            index = outer * step + k
            for part in range(rows // tall):
                row = messages[index, :, part * 128 : (part + 1) * 128]
                column = jnp.sum(jnp.where(lanes == offset, row, 0.0), axis=1, keepdims=True)
                decays[index, part * tall : (part + 1) * tall, :] = jnp.broadcast_to(
                    column, (tall, 128)
                )
        return 0

    lax.fori_loop(0, n // step, spread, 0)
    whole(parts, n - 1, recv_sem.at[1])

    def scan(outer, carry):
        running, kept = carry
        for k in range(step):
            index = outer * step + k
            running = jnp.where(starts_prompt(index, ends), zero, running)
            back[index] = running.astype(jnp.bfloat16)
            running = decays[index] * running + parts[index].astype(jnp.float32)
            kept = tuple(
                jnp.where(index == end - 1, running, final) for end, final in zip(ends, kept)
            )
        return running, kept

    _, kept = lax.fori_loop(0, n // step, scan, (zero, (zero,) * len(ends)))
    around(n, me, lambda peer: back_to(peer).start())
    for p, final in enumerate(kept):
        finals[p] = final.astype(jnp.bfloat16)
    around(levels, level, lambda other: finals_to(other).start()) if levels > 1 else None
    incoming[my_block] = back[me]
    all_finals[level] = finals[...]

    if levels > 1:
        whole(edges, levels - 1, recv_sem.at[2])
    ending = [jnp.zeros(edge_ref.shape, jnp.float32)] * len(ends)
    for upper in range(levels):
        held = edges[upper].astype(jnp.float32)
        for p, end in enumerate(ends):
            ending[p] = jnp.where(upper * group + member == end - 1, held, ending[p])
    edge_lanes = edge_ref.shape[1] // 128

    def wanted_by(other, slot):
        return messages[first_of_group + other, :, wide + 128 * slot : wide + 128 * (slot + 1)]

    def pick_edges(other):
        for slot in range(slots):
            wanted = jnp.concatenate([wanted_by(other, slot)] * edge_lanes, axis=1)
            picked = jnp.zeros(edge_ref.shape, jnp.float32)
            for p in range(len(ends)):
                picked = jnp.where(wanted == float(p), ending[p], picked)
            picked_edges[other, slot] = picked.astype(jnp.bfloat16)

    def pick_states(other):
        for slot in range(slots):
            wanted = wanted_by(other, slot)
            for upper in range(levels):
                picked = zero
                for p in range(len(ends)):
                    held = all_finals[upper, p].astype(jnp.float32)
                    picked = jnp.where(wanted == float(p), held, picked)
                handed[other, slot, upper] = picked.astype(jnp.bfloat16)

    def hand_edges(hop, _):
        other = lax.rem(member + hop, group)
        pick_edges(other)

        @pl.when(hop > 0)
        def _():
            picked_to(other).start()

        return 0

    lax.fori_loop(0, group, hand_edges, 0)
    owned_edges[member] = picked_edges[member]

    share = mixed_ref.shape[0]
    half = share // 2
    lower, upper_half = pl.ds(0, half), pl.ds(half, half)

    def partial_of(quarter):
        here = pl.ds(pl.multiple_of(quarter * share, share), share)
        skipped = pl.ds(pl.multiple_of(quarter * share + HALO, HALO), share)
        attended = local[here, :] + jnp.dot(
            query[here, :], incoming[...], preferred_element_type=jnp.float32
        )
        mean_square = jnp.mean(attended * attended, axis=1, keepdims=True)
        gate_values = gate[skipped, :].astype(jnp.float32)
        gated = (
            attended
            * lax.rsqrt(mean_square + EPS_HEAD)
            * head_gain_ref[...]
            * (gate_values * jax.nn.sigmoid(gate_values))
        ).astype(jnp.bfloat16)
        return jnp.dot(gated, w_out[...], preferred_element_type=jnp.float32).astype(jnp.bfloat16)

    def move(src, dst, to, index, recv):
        return pltpu.make_async_remote_copy(
            src_ref=src,
            dst_ref=dst,
            send_sem=send_sum.at[index],
            recv_sem=recv,
            device_id={"tensor": to},
            device_id_type=MESH,
        )

    moves = [
        move(to_far.at[lower], relay_right, left, 0, recv_relay.at[0]),
        move(to_far.at[upper_half], relay_left, right, 1, recv_relay.at[1]),
        move(to_left.at[upper_half], sum_right.at[upper_half], left, 2, recv_sum.at[0]),
        move(to_right.at[lower], sum_left.at[lower], right, 3, recv_sum.at[1]),
        move(to_left.at[lower], sum_right.at[lower], left, 4, recv_sum.at[2]),
        move(to_right.at[upper_half], sum_left.at[upper_half], right, 5, recv_sum.at[3]),
    ]
    whole(back, n - 1, recv_sem.at[4])
    to_far[...] = partial_of(far)
    moves[0].start()
    moves[1].start()
    to_left[...] = partial_of(left)
    moves[2].start()
    to_right[...] = partial_of(right)
    moves[3].start()
    moves[0].wait_recv()
    to_left[lower, :] = (
        to_left[lower, :].astype(jnp.float32) + relay_right[...].astype(jnp.float32)
    ).astype(jnp.bfloat16)
    moves[4].start()
    moves[1].wait_recv()
    to_right[upper_half, :] = (
        to_right[upper_half, :].astype(jnp.float32) + relay_left[...].astype(jnp.float32)
    ).astype(jnp.bfloat16)
    moves[5].start()

    if levels > 1:
        whole(all_finals, levels - 1, recv_sem.at[5])

    def hand_states(hop, _):
        other = lax.rem(member + hop, group)
        pick_states(other)

        @pl.when(hop > 0)
        def _():
            handed_to(other).start()

        return 0

    lax.fori_loop(0, group, hand_states, 0)
    owned[mine] = handed[member]

    for copy in moves[:2]:
        copy.wait_send()
    to_far[...] = partial_of(x)
    whole(owned_edges, group - 1, recv_sem.at[3])
    total = owned_edges[0].astype(jnp.float32)
    for other in range(1, group):
        total = total + owned_edges[other].astype(jnp.float32)
    owned_edge_ref[...] = total.astype(jnp.bfloat16)
    whole(handed, group - 1, recv_sem.at[6])
    owned_ref[...] = owned[...]
    for copy in moves[2:]:
        copy.wait_recv()
    row_of = x * share + lax.broadcasted_iota(jnp.int32, (share, 1), 0)
    summed = (
        to_far[...].astype(jnp.float32)
        + sum_right[...].astype(jnp.float32)
        + sum_left[...].astype(jnp.float32)
    )
    live = live_rows_of(me, ends, fills_ref, local.shape[0])
    mixed_ref[...] = jnp.where(row_of < live, summed, 0.0).astype(jnp.bfloat16)
    for copy in moves[2:]:
        copy.wait_send()
    whole(messages, n - 1, send_sem.at[0])
    whole(parts, n - 1, send_sem.at[1])
    whole(back, n - 1, send_sem.at[4])
    whole(owned_edges, group - 1, send_sem.at[3])
    whole(handed, group - 1, send_sem.at[6])
    if levels > 1:
        whole(edges, levels - 1, send_sem.at[2])
        whole(all_finals, levels - 1, send_sem.at[5])


def handoff(
    spans,
    fills,
    wanted,
    state,
    decay,
    edge,
    head_gain,
    local_out,
    query_decayed,
    gate_values,
    w_out,
):
    n = lax.axis_size("seq")
    group = 8 if n >= 64 else 4
    levels = n // group
    keys, values = state.shape
    slots, prompts = wanted.shape[0], spans.shape[0]
    lane_blocks = values // 128
    rows = keys * lane_blocks // n
    share = local_out.shape[0] // lax.axis_size("tensor")
    width = w_out.shape[1]
    wide = max(rows, 128)
    vmem = pl.BlockSpec(memory_space=pltpu.VMEM)
    smem = pl.BlockSpec(memory_space=pltpu.SMEM)
    half = jnp.bfloat16
    owned_shape = (slots, levels, group // lane_blocks, rows, values)
    return pl.pallas_call(
        functools.partial(handoff_kernel, n, group, rows),
        out_shape=(
            jax.ShapeDtypeStruct((share, width), half),
            jax.ShapeDtypeStruct(owned_shape, half),
            jax.ShapeDtypeStruct((slots,) + edge.shape, half),
        ),
        in_specs=[smem] * 3 + [vmem] * 8,
        out_specs=(vmem,) * 3,
        scratch_shapes=[
            pltpu.VMEM((keys // wide, 1, wide + 128 * slots), jnp.float32),
            pltpu.VMEM((n, rows, 128), half),
            pltpu.VMEM((n, 1, wide + 128 * slots), jnp.float32),
            pltpu.VMEM((n, rows, 128), jnp.float32),
            pltpu.VMEM((n, rows, 128), half),
            pltpu.VMEM((keys, values), half),
            pltpu.VMEM((prompts, rows, 128), half),
            pltpu.VMEM((levels, prompts, rows, 128), half),
            pltpu.VMEM((group, slots, levels, rows, 128), half),
            pltpu.VMEM(owned_shape, half),
            pltpu.VMEM((levels,) + edge.shape, half),
            pltpu.VMEM((group, slots) + edge.shape, half),
            pltpu.VMEM((group, slots) + edge.shape, half),
        ]
        + [pltpu.VMEM((share, width), half)] * 3
        + [pltpu.VMEM((share // 2, width), half)] * 2
        + [pltpu.VMEM((share, width), half)] * 2
        + [
            pltpu.SemaphoreType.DMA((7,)),
            pltpu.SemaphoreType.DMA((7,)),
            pltpu.SemaphoreType.DMA((6,)),
            pltpu.SemaphoreType.DMA((2,)),
            pltpu.SemaphoreType.DMA((4,)),
        ],
        compiler_params=pltpu.CompilerParams(
            collective_id=0, has_side_effects=True, vmem_limit_bytes=24 * 1024 * 1024
        ),
        name="state_handoff",
    )(
        spans,
        fills,
        wanted,
        state,
        decay,
        edge,
        head_gain.reshape(1, -1),
        local_out,
        query_decayed,
        gate_values,
        w_out,
    )


def local_kernel(
    spans_ref,
    fills_ref,
    projected_ref,
    low_rank_ref,
    gate_up_wide_ref,
    gate_bias_ref,
    conv_ref,
    out_ref,
    query_ref,
    state_ref,
    decay_ref,
    edge_ref,
    state,
    offset,
    gate_up_ref,
):
    live = live_rows_of(
        lax.axis_index("seq"), prompt_edges(spans_ref), fills_ref, out_ref.shape[0]
    )
    for rank in range(gate_up_ref.shape[0]):
        gate_up_ref[rank : rank + 1, :] = gate_up_wide_ref[rank]
    rows = out_ref.shape[0]
    keys, values = state.shape
    halo = projected_ref.shape[0] - rows
    taps = conv_ref.shape[0]
    state[...] = jnp.zeros_like(state)
    offset[...] = jnp.zeros_like(offset)
    row_of = lax.broadcasted_iota(jnp.int32, (STRETCH, 1), 0)
    at_row = lax.broadcasted_iota(jnp.int32, (STRETCH, STRETCH), 0)
    at_col = lax.broadcasted_iota(jnp.int32, (STRETCH, STRETCH), 1)
    lower = (at_row >= at_col).astype(jnp.float32)
    ones = jnp.ones((STRETCH, 128), jnp.float32)

    def contract(a, b, dims, precision=None):
        return lax.dot_general(
            a, b, (dims, ((), ())), precision=precision, preferred_element_type=jnp.float32
        )

    def one_block(block, _):
        base = pl.multiple_of(block * STRETCH, STRETCH)
        here = pl.ds(base, STRETCH)
        window = projected_ref[pl.ds(base, STRETCH + halo), :].astype(jnp.float32)
        total = jnp.zeros((STRETCH, window.shape[1]), jnp.float32)
        for tap in range(taps):
            first = halo - taps + 1 + tap
            total = total + conv_ref[tap] * window[first : first + STRETCH]
        activated = (total * jax.nn.sigmoid(total)).astype(jnp.bfloat16)
        valid = base + row_of < live
        query = activated[:, :keys].astype(jnp.float32) * keys ** (-0.5)
        key = jnp.where(valid, activated[:, keys : 2 * keys].astype(jnp.float32), 0.0)
        value = activated[:, 2 * keys :]
        logits = contract(
            low_rank_ref[pl.ds(base + halo, STRETCH), :], gate_up_ref[...], ((1,), (0,)), EXACT_MATMUL
        ) + gate_bias_ref[...]
        log_decay = (jnp.minimum(logits, 0.0) - jnp.log1p(jnp.exp(-jnp.abs(logits)))) / 16.0
        log_decay = jnp.where(valid, log_decay, 0.0)
        running = contract(lower, log_decay, ((1,), (0,)), EXACT_MATMUL)
        closing = running[STRETCH - 1 : STRETCH]
        closing_column = contract(log_decay, ones, ((0,), (0,)), EXACT_MATMUL)

        scores = jnp.zeros((STRETCH, STRETCH), jnp.float32)
        half = STRETCH // 2
        while half >= 8:
            pair = 2 * half
            pieces = []
            for first in range(0, STRETCH, pair):
                middle = running[first + half - 1 : first + half]
                pieces.append(jnp.broadcast_to(middle, (pair, keys)))
            middle = pieces[0] if len(pieces) == 1 else jnp.concatenate(pieces, axis=0)
            factor = jnp.exp(-jnp.abs(running - middle))
            second = row_of % pair >= half
            left = jnp.where(second, query * factor, 0.0).astype(jnp.bfloat16)
            right = jnp.where(second, 0.0, key * factor).astype(jnp.bfloat16)
            part = contract(left, right, ((1,), (1,)))
            scores = scores + jnp.where(at_row // pair == at_col // pair, part, 0.0)
            half //= 2
        for shift in range(8):
            if shift:
                moved_key = pltpu.roll(key, shift, 0)
                moved_sum = pltpu.roll(running, shift, 0)
                product = query * moved_key * jnp.exp(jnp.minimum(running - moved_sum, 0.0))
            else:
                product = query * key
            summed = jnp.sum(product, axis=1, keepdims=True)
            chosen = (at_col == at_row - shift) & (at_row % 8 >= shift)
            scores = scores + jnp.where(chosen, summed, 0.0)

        decayed = (query * jnp.exp(running)).astype(jnp.bfloat16)
        weighted = (key * jnp.exp(closing - running)).astype(jnp.bfloat16)
        query_ref[here, :] = (query * jnp.exp(running + offset[...])).astype(jnp.bfloat16)
        before = state[...]
        out_ref[here, :] = contract(
            scores.astype(jnp.bfloat16), value, ((1,), (0,))
        ) + contract(decayed, before.astype(jnp.bfloat16), ((1,), (0,)))
        factor = jnp.exp(closing_column)
        factor = jnp.concatenate([factor] * (values // 128), axis=1)
        state[...] = factor * before + contract(weighted, value, ((0,), (0,)))
        offset[...] = offset[...] + closing
        return 0

    lax.fori_loop(0, rows // STRETCH, one_block, 0)
    state_ref[...] = state[...].astype(jnp.bfloat16)
    decay_ref[...] = jnp.exp(offset[...])
    first = live + halo - taps + 1
    base = pl.multiple_of(jnp.minimum(first // 16 * 16, rows + halo - 32), 16)
    window = projected_ref[pl.ds(base, 32), :]
    wanted = lax.broadcasted_iota(jnp.int32, (8, 32), 0) + (first - base)
    here = lax.broadcasted_iota(jnp.int32, (8, 32), 1)
    chosen = (wanted == here).astype(jnp.bfloat16)
    edge_ref[...] = contract(chosen, window, ((1,), (0,))).astype(jnp.bfloat16)


def local_blocks(spans, fills, projected, low_rank, gate_up, gate_bias, conv_weight, values):
    rows = low_rank.shape[0] - HALO
    keys = gate_up.shape[2]
    vmem = pl.BlockSpec(memory_space=pltpu.VMEM)
    smem = pl.BlockSpec(memory_space=pltpu.SMEM)
    return pl.pallas_call(
        local_kernel,
        out_shape=(
            jax.ShapeDtypeStruct((rows, values), jnp.float32),
            jax.ShapeDtypeStruct((rows, keys), jnp.bfloat16),
            jax.ShapeDtypeStruct((keys, values), jnp.bfloat16),
            jax.ShapeDtypeStruct((1, keys), jnp.float32),
            jax.ShapeDtypeStruct((8, projected.shape[1]), jnp.bfloat16),
        ),
        in_specs=[smem, smem] + [vmem] * 5,
        out_specs=(vmem,) * 5,
        scratch_shapes=[
            pltpu.VMEM((keys, values), jnp.float32),
            pltpu.VMEM((1, keys), jnp.float32),
            pltpu.VMEM((gate_up.shape[0], keys), jnp.float32),
        ],
        compiler_params=pltpu.CompilerParams(vmem_limit_bytes=20 * 1024 * 1024),
        name="local_blocks",
    )(spans, fills, projected, low_rank, gate_up, gate_bias, conv_weight)


def body(
    tokens,
    norm_gain,
    w_qkv,
    w_gate_out,
    gate_down,
    gate_up,
    gate_bias,
    conv_weight,
    head_gain,
    w_out,
    spans,
    fills,
    request_prompt,
):
    model_width, local_heads, width_qkv = w_qkv.shape
    value_width = head_gain.shape[0]
    key_width = gate_up.shape[2]
    taps = conv_weight.shape[0]
    slot_count = request_prompt.shape[0]
    flat_qkv = w_qkv.reshape(model_width, local_heads * width_qkv)
    extended, gate_values, low_rank = project(
        spans, tokens, norm_gain, flat_qkv, w_gate_out, gate_down
    )
    local_out, query_decayed, local_state, decay, edge = local_blocks(
        spans, fills, extended, low_rank, gate_up, gate_bias, conv_weight, value_width
    )
    mixed, owned_state, owned_edge = handoff(
        spans,
        fills,
        request_prompt,
        local_state,
        decay,
        edge,
        head_gain,
        local_out,
        query_decayed,
        gate_values,
        w_out,
    )
    owner_state = owned_state.reshape(slot_count, local_heads, key_width, value_width).astype(
        jnp.float32
    )
    owner_edge = owned_edge[:, : taps - 1].reshape(slot_count, taps - 1, local_heads, width_qkv)
    return (mixed, owner_state, owner_edge)


def solution(mesh):
    return jax.shard_map(
        body,
        mesh=mesh,
        in_specs=(
            P("seq", "tensor"),
            P(),
            P(None, "tensor", None),
            P(None, "tensor"),
            P(),
            P(None, "tensor", None),
            P("tensor", None),
            P(None, "tensor", None),
            P(),
            P("tensor", None),
            P(),
            P(),
            P("seq"),
        ),
        out_specs=(
            P(("seq", "tensor"), None),
            P("seq", "tensor", None, None),
            P("seq", None, "tensor", None),
        ),
        check_vma=False,
    )
```

time: 131 us -> 96.8 us (0.74)
  the two profiles are of different devices: /device:TPU:241 before, /device:TPU:1 now
where the time goes in v4:
time: 96.8 us; the launch traced here: 96.7 us
  Pallas kernels  92.8 us (96%)
  local copies, waits for them, and re-layouts  2.09 us (2%)
  other arithmetic  1.1 us (1%)
    pallas_call x1, Pallas kernels, handoff(): pl.pallas_call(functools.partial(handoff_kernel, n, group, rows), out_sha...  53.7 us
    pallas_call x1, Pallas kernels, project(): pl.pallas_call(project_kernel, out_shape=(jax.ShapeDtypeStruct((tall, w_q...  28 us
    pallas_call x1, Pallas kernels, local_blocks(): pl.pallas_call(local_kernel, out_shape=(jax.ShapeDtypeStruct((rows, value...  11.1 us
    unnamed x20, local copies, waits for them, and re-layouts  2.09 us

profile of v4, /device:TPU:1, one launch (start us, length us, event | category | flops | bytes accessed | tf_op | source)
XLA Modules:
  0.0 96.7 jit_solution(2499063335333393981)
XLA Ops:
  0.6 0.0 copy-start.3
  0.6 0.6 copy-done.3
  1.3 0.0 copy-start.1
  1.3 0.0 copy-start.2
  1.3 0.0 copy-start.6
  1.3 0.0 copy-start.7
  1.3 0.0 copy-start
  1.3 0.0 copy-start.4
  1.3 0.0 copy-start.5
  1.3 0.0 copy-start.8
  1.3 28.0 %gather_project.1 = (bf16[528,1024]{1,0:T(8,128)(2,1)S(1)}, bf16[528,512]{1,0:T(8,128)(2,1)S(1)}, f32[528,16]{1,0:T(8,128)S(1)}) custom-call(s32[3]{0:T(128)S(1)} %copy-done.3, bf16[512,512]{1,0:T(8,128)(2,1)} %tokens_ref.1, f32[1,2048]{1,0:T(1,128)} %bitcast.15, bf16[2048,1024]{1,0:T(8,128)(2,1)} %bitcast.13, bf16[2048,512]{1,0:T(8,128)(2,1)} %gate_hbm.1, ...), custom_call_target="tpu_custom_call" | custom-call | tf_op jit(solution)/shard_map/gather_project/pallas_call | solution.py:217
  29.3 0.0 copy-done.1
  29.4 0.0 copy-done.2
  29.4 0.0 copy-done.6
  29.4 0.0 copy-done.7
  29.4 11.1 %local_blocks.1 = (f32[512,512]{1,0:T(8,128)S(1)}, bf16[512,256]{1,0:T(8,128)(2,1)S(1)}, bf16[256,512]{1,0:T(8,128)(2,1)S(1)}, f32[1,256]{1,0:T(1,128)S(1)}, bf16[8,1024]{1,0:T(8,128)(2,1)S(1)}) custom-call(s32[3]{0:T(128)S(1)} %copy-done.3, s32[3]{0:T(128)S(1)} %copy-done.6, bf16[528,1024]{1,0:T(8,128)(2,1)S(1)} %get-tuple-element.14.projected_ref, ...), custom_call_target="tpu_custom_call" | custom-call | tf_op jit(solution)/shard_map/local_blocks/pallas_call | solution.py:782
  40.5 0.0 copy-done
  40.5 0.0 copy-done.4
  40.5 0.0 copy-done.5
  40.5 0.0 copy-done.8
  40.5 53.7 %state_handoff.1 = (bf16[128,2048]{1,0:T(8,128)(2,1)S(1)}, bf16[2,8,2,16,512]{4,3,2,1,0:T(8,128)(2,1)S(1)}, bf16[2,8,1024]{2,1,0:T(8,128)(2,1)S(1)}) custom-call(s32[3]{0:T(128)S(1)} %copy-done.4, s32[3]{0:T(128)S(1)} %copy-done.6, s32[2]{0:T(128)S(1)} %copy-done.8, bf16[256,512]{1,0:T(8,128)(2,1)S(1)} %get-tuple-element.16.state_ref, ...), custom_call_target="tpu_custom_call" | custom-call | tf_op jit(solution)/shard_map/state_handoff/pallas_call | solution.py:611
  94.2 0.6 copy.17
  94.8 1.1 %convert.2 = f32[2,1,256,512]{3,2,1,0:T(8,128)} convert(bf16[2,1,256,512]{3,2,1,0:T(8,128)(2,1)S(1)} %bitcast.11) | non-fusion elementwise | flops 262144 | bytes 1572864
  95.9 0.8 copy.19
  (1 shorter events, 0.0 us)
Async XLA Ops:
  0.6 0.7 copy-start.3
  1.3 28.1 %copy-start.1 = (f32[16,1,256]{2,1,0:T(1,128)S(1)}, f32[16,1,256]{2,1,0:T(1,128)}, u32[]{:S(2)}) copy-start(f32[16,1,256]{2,1,0:T(1,128)} %gate_up_wide_ref.1) | copy-start | bytes 49156
  1.3 28.1 %copy-start.2 = (f32[4,1,1024]{2,1,0:T(1,128)S(1)}, f32[4,1,1024]{2,1,0:T(1,128)}, u32[]{:S(2)}) copy-start(f32[4,1,1024]{2,1,0:T(1,128)} %conv_ref.1) | copy-start | bytes 49156
  1.3 28.1 %copy-start.6 = (s32[3]{0:T(128)S(1)}, s32[3]{0:T(128)}, u32[]{:S(2)}) copy-start(s32[3]{0:T(128)} %fills_ref.3) | copy-start | bytes 40
  1.3 28.1 %copy-start.7 = (f32[1,256]{1,0:T(1,128)S(1)}, f32[1,256]{1,0:T(1,128)}, u32[]{:S(2)}) copy-start(f32[1,256]{1,0:T(1,128)} %gate_bias_ref.1) | copy-start | bytes 3076
  1.3 39.2 %copy-start = (bf16[512,2048]{1,0:T(8,128)(2,1)S(1)}, bf16[512,2048]{1,0:T(8,128)(2,1)}, u32[]{:S(2)}) copy-start(bf16[512,2048]{1,0:T(8,128)(2,1)} %w_out.1) | copy-start | bytes 6291460
  1.3 39.2 %copy-start.4 = (s32[3]{0:T(128)S(1)}, s32[3]{0:T(128)}, u32[]{:S(2)}) copy-start(s32[3]{0:T(128)} %spans_ref.5) | copy-start | bytes 40
  1.3 39.2 %copy-start.5 = (f32[512]{0:T(512)S(1)}, f32[512]{0:T(512)}, u32[]{:S(2)}) copy-start(f32[512]{0:T(512)} %param.21) | copy-start | bytes 6148
  1.3 39.2 %copy-start.8 = (s32[2]{0:T(128)S(1)}, s32[2]{0:T(128)}, u32[]{:S(2)}) copy-start(s32[2]{0:T(128)} %request_ref.1) | copy-start | bytes 28
